TPU v7x, 128 devices: a whole 4x4x4 slice. The times are simulated.
128 devices in a mesh: ctx: 32 (over y, x, core), mix: 4 (over z).
Axes of the slice: x: 4, y: 4, z: 4, core: 2. Of those that a mesh axis runs over, the one named last changes fastest.
Arguments:
- sources: float32 [16, 262144], P('mix', 'ctx'), may hold values from -6 to 6
- source_ids: int32 [8, 3], replicated, may hold values from 0 to 15
- mix_weights: float32 [8, 3], replicated, may hold values from 0.1 to 0.8, as said below
- source_lengths: int32 [8, 3], replicated, may hold values from 1024 to 8192, as said below
- w_embed: bfloat16 [512, 32], replicated, may hold values from -1 to 1
- w_qkv: bfloat16 [512, 1536], replicated, may hold values from -0.25 to 0.25
- w_out: bfloat16 [512, 512], replicated, may hold values from -0.25 to 0.25
- forget: float32 [8, 4, 8192], P('mix', None, 'ctx'), may hold values from 0.5 to 1, as said below
- cotangent: bfloat16 [8, 8192, 512], P('mix', 'ctx'), may hold values from -0.0625 to 0.0625
Outputs:
- output: bfloat16 [8, 8192, 512], P('mix', 'ctx')
- grad_qkv: float32 [512, 1536], P('ctx')
- grad_out: float32 [512, 512], P('ctx')
- grad_embed: float32 [512, 32], P('ctx')
Inputs may be any that keep to these rules, and one draw needn't show every extreme that they name: `mix_weights`: each row sums to one. `source_lengths`: in every row one entry equals 8192. `forget`: below one.
All inputs are finite; a program needn't handle non-finite values.
Results may differ from a plain program's by a relative error of at most 0.015.
Values sent between devices are 32-bit elements; how exact they have to be, the bound alone decides.
A program may use at most 128 MiB of HBM per device.

v0:
```python
import jax
import jax.numpy as jnp
from jax import lax
from jax.sharding import PartitionSpec as P

SPAN = 256


EPS = 1e-06


def prefix(part, axis, combine, identity, reverse):
    count = lax.axis_size(axis)
    place = lax.axis_index(axis)
    ahead = count - 1 - place if reverse else place
    gathered = jax.tree.map(lambda a: lax.all_gather(a, axis), part)
    state = jax.tree.map(lambda a, e: jnp.zeros_like(a) + jnp.asarray(e, a.dtype), part, identity)

    def one(hop, state):
        source = count - 1 - hop if reverse else hop
        return combine(
            state, jax.tree.map(lambda a: lax.dynamic_index_in_dim(a, source, 0, False), gathered)
        )

    return lax.fori_loop(0, ahead, one, state)


def product(spec, left, right):
    return jnp.einsum(spec, left, right, preferred_element_type=jnp.float32)


def scaled(array, factor):
    return (array.astype(jnp.float32) * factor[..., None]).astype(jnp.bfloat16)


def causal_decay(cumulative):
    length = cumulative.shape[-1]
    causal = jnp.arange(length)[:, None] >= jnp.arange(length)[None, :]
    return jnp.where(causal, jnp.exp(cumulative[..., :, None] - cumulative[..., None, :]), 0.0)


def block_forward(queries, key_rows, value_rows, log_gate, memory):
    cumulative = jnp.cumsum(log_gate, axis=-1)
    final = cumulative[..., -1:]
    decay_mask = causal_decay(cumulative)
    from_memory = product(
        "bhcd,bhde->bhce", scaled(queries, jnp.exp(cumulative)), memory.astype(jnp.bfloat16)
    )
    weights = (product("bhcd,bhsd->bhcs", queries, key_rows) * decay_mask).astype(jnp.bfloat16)
    inside = product("bhcs,bhse->bhce", weights, value_rows)
    written = product("bhcd,bhce->bhde", scaled(key_rows, jnp.exp(final - cumulative)), value_rows)
    updated = jnp.exp(final)[..., None] * memory + written
    return (from_memory + inside, updated)


def block_backward(queries, key_rows, value_rows, grad_read, log_gate, memory, later):
    cumulative = jnp.cumsum(log_gate, axis=-1)
    final = cumulative[..., -1:]
    decay_mask = causal_decay(cumulative)
    growth = jnp.exp(cumulative)
    decay_factor = jnp.exp(final - cumulative)
    left = (product("bhce,bhse->bhcs", grad_read, value_rows) * decay_mask).astype(jnp.bfloat16)
    right = (product("bhcd,bhsd->bhcs", queries, key_rows) * decay_mask).astype(jnp.bfloat16)
    later_half = later.astype(jnp.bfloat16)
    grad_query = product(
        "bhce,bhde->bhcd", scaled(grad_read, growth), memory.astype(jnp.bfloat16)
    ) + product("bhcs,bhsd->bhcd", left, key_rows)
    grad_key = product("bhcs,bhcd->bhsd", left, queries) + product(
        "bhse,bhde->bhsd", scaled(value_rows, decay_factor), later_half
    )
    grad_value = product("bhcs,bhce->bhse", right, grad_read) + product(
        "bhsd,bhde->bhse", scaled(key_rows, decay_factor), later_half
    )
    earlier = jnp.exp(final)[..., None] * later + product(
        "bhcd,bhce->bhde", scaled(queries, growth), grad_read
    )
    return (grad_query, grad_key, grad_value, earlier)


def to_blocks(array):
    shaped = array.reshape(array.shape[:2] + (array.shape[2] // SPAN, SPAN) + array.shape[3:])
    return jnp.moveaxis(shaped, 2, 0)


def from_blocks(blocked):
    moved = jnp.moveaxis(blocked, 0, 2)
    return moved.reshape(moved.shape[:2] + (moved.shape[2] * moved.shape[3],) + moved.shape[4:])


def forward_combine(earlier, later):
    return (earlier[0] * later[0], later[0][..., None, None] * earlier[1] + later[1])


def reverse_merge(earlier, later):
    return (later[0] * earlier[0], later[1] + later[0][..., None, None] * earlier[1])


def carry_forward(decays, ends):
    identity = (jnp.ones_like(decays), jnp.zeros_like(ends))
    return prefix((decays, ends), "ctx", forward_combine, identity, False)[1]


def carry_backward(decays, starts):
    identity = (jnp.ones_like(decays), jnp.zeros_like(starts))
    return prefix((decays, starts), "ctx", reverse_merge, identity, True)[1]


def contract_rows(left, right):
    return lax.dot_general(
        left, right, (((0,), (0,)), ((), ())), preferred_element_type=jnp.float32
    )


def contract_cols(left, right):
    return lax.dot_general(
        left, right, (((1,), (1,)), ((), ())), preferred_element_type=jnp.float32
    )


def shards(
    sources, source_ids, mix_weights, source_lengths, w_embed, w_qkv, w_out, forget, cotangent
):
    mix_index = lax.axis_index("mix")
    ctx_index = lax.axis_index("ctx")
    patch_size = w_embed.shape[1]
    steps_dev = sources.shape[1] // patch_size
    local_mix = forget.shape[0]
    head_count = forget.shape[1]
    width = w_qkv.shape[0]
    head_size = width // head_count
    row_count = local_mix * steps_dev
    positions = ctx_index * steps_dev + jnp.arange(steps_dev, dtype=jnp.int32)
    all_sources = lax.all_gather(sources, "mix", axis=0, tiled=True)
    own_ids = lax.dynamic_slice_in_dim(source_ids, mix_index * local_mix, local_mix, 0)
    own_weights = lax.dynamic_slice_in_dim(mix_weights, mix_index * local_mix, local_mix, 0)
    own_lengths = lax.dynamic_slice_in_dim(source_lengths, mix_index * local_mix, local_mix, 0)
    mixture = jnp.zeros((local_mix, steps_dev, patch_size), jnp.float32)
    for term in range(source_ids.shape[1]):
        chosen = jnp.take(all_sources, own_ids[:, term], axis=0).reshape(
            local_mix, steps_dev, patch_size
        )
        cover = jnp.where(
            positions[None, :] < own_lengths[:, term : term + 1],
            own_weights[:, term : term + 1],
            0.0,
        )
        mixture = mixture + cover[:, :, None] * chosen
    mixture_half = mixture.reshape(row_count, patch_size).astype(jnp.bfloat16)
    embedded = contract_cols(mixture_half, w_embed).astype(jnp.bfloat16)
    projected = jnp.dot(embedded, w_qkv, preferred_element_type=jnp.float32).astype(jnp.bfloat16)
    parts = projected.reshape(local_mix, steps_dev, 3, head_count, head_size).transpose(
        2, 0, 3, 1, 4
    )
    queries = parts[0]
    key_rows = parts[1]
    value_rows = parts[2]
    log_gate = jnp.log1p(forget - 1.0)
    device_cumulative = jnp.cumsum(log_gate, axis=-1)
    device_total = device_cumulative[..., -1]
    device_decay = jnp.exp(device_total)
    growth = jnp.exp(device_cumulative)
    decay_factor = jnp.exp(device_total[..., None] - device_cumulative)
    query_blocks = to_blocks(queries)
    key_blocks = to_blocks(key_rows)
    value_blocks = to_blocks(value_rows)
    gate_blocks = to_blocks(log_gate)

    def forward_step(memory, inputs_block):
        read_block, updated = block_forward(
            inputs_block[0], inputs_block[1], inputs_block[2], inputs_block[3], memory
        )
        return (updated, (read_block, memory))

    local_end = product("bhtd,bhte->bhde", scaled(key_rows, decay_factor), value_rows)
    incoming = carry_forward(device_decay, local_end)
    last_state, (read_blocks, block_states) = lax.scan(
        forward_step, incoming, (query_blocks, key_blocks, value_blocks, gate_blocks)
    )
    read = from_blocks(read_blocks)
    inverse_rms = lax.rsqrt(jnp.mean(read * read, axis=-1, keepdims=True) + EPS)
    normed = read * inverse_rms
    normed_half = normed.transpose(0, 2, 1, 3).reshape(row_count, width).astype(jnp.bfloat16)
    output = jnp.dot(normed_half, w_out, preferred_element_type=jnp.float32).astype(jnp.bfloat16)
    grad_rows_in = cotangent.reshape(row_count, width)
    grad_out = contract_rows(normed_half, grad_rows_in)
    grad_normed = (
        contract_cols(grad_rows_in, w_out)
        .reshape(local_mix, steps_dev, head_count, head_size)
        .transpose(0, 2, 1, 3)
    )
    grad_read = (
        inverse_rms
        * (grad_normed - normed * jnp.mean(grad_normed * normed, axis=-1, keepdims=True))
    ).astype(jnp.bfloat16)

    def backward_step(later, inputs_block):
        grad_query, grad_key, grad_value, earlier = block_backward(
            inputs_block[0],
            inputs_block[1],
            inputs_block[2],
            inputs_block[3],
            inputs_block[4],
            inputs_block[5],
            later,
        )
        return (earlier, (grad_query, grad_key, grad_value))

    backward_inputs = (
        query_blocks,
        key_blocks,
        value_blocks,
        to_blocks(grad_read),
        gate_blocks,
        block_states,
    )
    local_start = product("bhtd,bhte->bhde", scaled(queries, growth), grad_read)
    outgoing = carry_backward(device_decay, local_start)
    first_back, (query_grads, key_grads, value_grads) = lax.scan(
        backward_step, outgoing, backward_inputs, reverse=True
    )
    grad_query = from_blocks(query_grads)
    grad_key = from_blocks(key_grads)
    grad_value = from_blocks(value_grads)
    stacked = jnp.stack([grad_query, grad_key, grad_value])
    grad_proj = stacked.transpose(1, 3, 0, 2, 4).reshape(row_count, 3 * width).astype(jnp.bfloat16)
    grad_qkv = contract_rows(embedded, grad_proj)
    grad_embedded = contract_cols(grad_proj, w_qkv).astype(jnp.bfloat16)
    grad_embed = contract_rows(grad_embedded, mixture_half)
    running_sums = lax.psum((grad_qkv, grad_out, grad_embed), "mix")
    result = (
        lax.psum_scatter(running_sums[0], "ctx", scatter_dimension=0, tiled=True),
        lax.psum_scatter(running_sums[1], "ctx", scatter_dimension=0, tiled=True),
        lax.psum_scatter(running_sums[2], "ctx", scatter_dimension=0, tiled=True),
    )
    return (output.reshape(local_mix, steps_dev, width), result[0], result[1], result[2])


def solution(mesh):
    placed = (
        P("mix", "ctx"),
        P(),
        P(),
        P(),
        P(),
        P(),
        P(),
        P("mix", None, "ctx"),
        P("mix", "ctx", None),
    )
    return jax.shard_map(
        shards,
        mesh=mesh,
        in_specs=placed,
        out_specs=(P("mix", "ctx", None), P("ctx", None), P("ctx", None), P("ctx", None)),
        check_vma=False,
    )
```

profile of v0, /device:TPU:1, one launch (start us, length us, event | category | flops | bytes accessed | tf_op | source)
XLA Modules:
  0.0 568.6 jit_solution(10031244796681342466)
XLA Ops:
  10.1 2.4 reduce-window.14
  13.2 13.6 %all-gather.3 = f32[4,4,8192]{2,1,0:T(4,128)S(1)} all-gather(f32[1,4,8192]{2,1,0:T(4,128)} %bitcast.165), channel_id=1, replica_groups=mesh['ctx'=32,'mix'=4] {'mix'}, dimensions={0}, use_global_device_ids=true | all-gather | bytes 655360 | tf_op jit(solution)/shard_map/all_gather | solution.py:133
  31.9 1.4 reshape.279
  33.3 1.7 copy.83
  35.0 1.6 fusion.19
  36.7 26.6 %all-gather = f32[64,4,1]{1,2,0:T(1,128)S(1)} all-gather(f32[2,4,1]{1,2,0:T(1,128)S(1)} %exp.49), channel_id=2, replica_groups=mesh['ctx'=32,'mix'=4] {'ctx'}, dimensions={0}, use_global_device_ids=true | all-gather | bytes 1056 | tf_op jit(solution)/shard_map/all_gather | solution.py:16
  63.3 1.5 multiply_convert_fusion.1
  64.8 48.0 %all-gather.7.cloned.1.call-done = f32[64,4,128,128]{3,2,1,0:T(8,128)} async-done(((f32[2,4,128,128]{3,2,1,0:T(8,128)}), f32[64,4,128,128]{3,2,1,0:T(8,128)}) %all-gather.7.cloned.1.call-update) | async-done | bytes 16777232 | tf_op jit(solution)/shard_map/all_gather | solution.py:16
  112.8 1.2 while.16
  114.1 1.6 fusion.18
  115.7 1.9 multiply_reduce_fusion.1
  119.9 1.6 fusion.17
  121.6 1.6 fusion.8
  123.9 1.2 fusion.5
  125.1 1.5 fusion.26
  126.6 1.5 fusion.20
  128.0 101.6 %all-gather.9.cloned.1.call-done = f32[64,4,128,128]{3,2,1,0:T(8,128)} async-done(((f32[2,4,128,128]{3,2,1,0:T(8,128)}), f32[64,4,128,128]{3,2,1,0:T(8,128)}) %all-gather.9.cloned.1.call-update) | async-done | bytes 16777232 | tf_op jit(solution)/shard_map/all_gather | solution.py:16
  229.7 37.1 %while.17 = (s32[]{:T(128)}, f32[2,4,128,128]{3,2,1,0:T(8,128)S(1)}, s32[]{:T(128)}, f32[32,2,4,128,128]{4,3,2,1,0:T(8,128)}, f32[32,2,4]{2,1,0:T(2,128)S(1)}, /*index=5*/s32[]{:T(128)}, s32[]{:T(128)}, s32[]{:T(128)}, s32[]{:T(128)}) while((s32[]{:T(128)}, f32[2,4,128,128]{3,2,1,0:T(8,128)S(1)}, s32[]{:T(128)}, ...), condition=%wide.region_7.9_spmd, body=%wide.region_6.8_spmd.sunk | while | flops 262150 | bytes 1573115 | solution.py:25
  266.8 1.9 fusion.3
  268.8 1.6 fusion.4
  270.5 2.4 copy.55
  272.9 3.9 convert_element_type.116
  276.8 4.1 fusion.27
  282.5 1.5 fusion.9
  284.1 2.1 fusion.6
  286.3 70.6 %reduce-scatter.4.cloned.1.call-done = f32[16,1536]{1,0:T(8,128)} async-done(((f32[512,1536]{1,0:T(8,128)}), f32[16,1536]{1,0:T(8,128)}) %reduce-scatter.4.cloned.1.call-update) | async-done | bytes 98320 | tf_op jit(solution)/shard_map/reduce_scatter | solution.py:231
  356.9 2.4 convolution_convert_fusion.2
  359.4 77.9 %reduce-scatter.6.cloned.1.call-done = f32[16,512]{1,0:T(8,128)} async-done(((f32[512,512]{1,0:T(8,128)}), f32[16,512]{1,0:T(8,128)}) %reduce-scatter.6.cloned.1.call-update) | async-done | bytes 32784 | tf_op jit(solution)/shard_map/reduce_scatter | solution.py:232
  437.2 79.8 %reduce-scatter.8.cloned.1.call-done = f32[16,32]{1,0:T(8,128)} async-done(((f32[512,32]{1,0:T(8,128)}), f32[16,32]{1,0:T(8,128)}) %reduce-scatter.8.cloned.1.call-update) | async-done | bytes 2064 | tf_op jit(solution)/shard_map/reduce_scatter | solution.py:233
  517.0 15.1 %all-reduce = (f32[16,512]{1,0:T(8,128)}, f32[16,32]{1,0:T(8,128)}) all-reduce(f32[16,512]{1,0:T(8,128)} %reduce-scatter.6.cloned.1.call-done, f32[16,32]{1,0:T(8,128)} %reduce-scatter.8.cloned.1.call-done), channel_id=1, replica_groups=mesh['ctx'=32,'mix'=4] {'mix'}, use_global_device_ids=true, to_apply=%region_10.12 | all-reduce | flops 8704 | bytes 69632 | tf_op jit(solution)/shard_map/psum | solution.py:229
  532.1 28.1 %all-reduce.3.cloned.1.call-done = f32[16,1536]{1,0:T(8,128)} async-done(((f32[16,1536]{1,0:T(8,128)}), f32[16,1536]{1,0:T(8,128)}) %all-reduce.3.cloned.1.call-update) | async-done | bytes 98320 | tf_op jit(solution)/shard_map/psum | solution.py:229
  560.2 1.5 copy.99
  (167 shorter events, 50.7 us)
Async XLA Ops:
  7.2 23.7 %copy-start = (bf16[512,1536]{1,0:T(8,128)(2,1)S(1)}, bf16[512,1536]{1,0:T(8,128)(2,1)}, u32[]{:S(2)}) copy-start(bf16[512,1536]{1,0:T(8,128)(2,1)} %param.20) | copy-start | bytes 4718596
  7.2 105.6 %all-gather.7.cloned.1.call-start = ((), (), s32[]{:S(2)}) async-start(), calls=%async_computation.3 | async-start | bytes 17301504 | tf_op jit(solution)/shard_map/all_gather | solution.py:16
  28.1 1.7 copy-start.16
  30.1 0.8 copy-start.9
  35.0 29.8 %copy-start.1 = (bf16[2,256,3,4,128]{4,1,3,0,2:T(8,128)(2,1)}, bf16[2,256,3,4,128]{4,1,3,0,2:T(8,128)(2,1)S(1)}, u32[]{:S(2)}) copy-start(bf16[2,256,3,4,128]{4,1,3,0,2:T(8,128)(2,1)S(1)} %copy.83) | copy-start | bytes 4718596
  36.6 193.0 %all-gather.9.cloned.1.call-start = ((), (), s32[]{:S(2)}) async-start(), calls=%async_computation.4 | async-start | bytes 17301504 | tf_op jit(solution)/shard_map/all_gather | solution.py:16
  114.1 1.6 copy-start.2
  115.7 1.9 copy-start.12
  115.7 1.9 copy-start.15
  119.1 0.8 copy-start.4
  121.5 235.4 %reduce-scatter.4.cloned.1.call-start = ((), (), s32[]{:S(2)}) async-start(), calls=%async_computation.5 | async-start | bytes 3244032 | tf_op jit(solution)/shard_map/reduce_scatter | solution.py:231
  121.6 1.7 copy-start.3
  121.6 1.7 copy-start.5
  123.9 1.2 copy-start.7
  266.8 2.0 copy-start.8
  268.8 1.6 copy-start.14
  272.9 3.9 copy-start.10
  280.9 156.3 %reduce-scatter.6.cloned.1.call-start = ((), (), s32[]{:S(2)}) async-start(), calls=%async_computation.7 | async-start | bytes 1081344 | tf_op jit(solution)/shard_map/reduce_scatter | solution.py:232
  280.9 1.6 copy-start.13
  281.7 0.8 copy-start.11
  282.5 1.5 copy-start.6
  284.0 233.0 %reduce-scatter.8.cloned.1.call-start = ((), (), s32[]{:S(2)}) async-start(), calls=%async_computation.8 | async-start | bytes 270336 | tf_op jit(solution)/shard_map/reduce_scatter | solution.py:233
  286.3 274.0 %all-reduce.3.cloned.1.call-start = ((), (), s32[]{:S(2)}) async-start(), calls=%async_computation.6 | async-start | bytes 196608 | tf_op jit(solution)/shard_map/psum | solution.py:229
Sparse Core Ops, SparseCore 0:
  36.8 75.9 all-gather.6
  121.7 107.9 all-gather.8
  281.0 75.8 reduce-scatter.3
  360.3 76.9 reduce-scatter.5
  440.5 76.4 reduce-scatter.7
  519.2 40.9 all-reduce.2
where the time goes:
time: 572 us; the launch traced here: 569 us
  waiting for transfers between devices  406 us (71%)
  blocking collectives  55.3 us (10%)
  other arithmetic  42.1 us (7%)
  matrix products  30.2 us (5%)
  local copies, waits for them, and re-layouts  19 us (3%)
  between operations  14.6 us (3%)
    all_gather x2, waiting for transfers between devices, prefix(): gathered = jax.tree.map(lambda a: lax.all_gather(a, axis), part)  150 us
    reduce_scatter x1, waiting for transfers between devices, shards(): lax.psum_scatter(running_sums[2], 'ctx', scatter_dimension=0, tiled=True)  79.8 us
    reduce_scatter x1, waiting for transfers between devices, shards(): lax.psum_scatter(running_sums[1], 'ctx', scatter_dimension=0, tiled=True)  77.9 us
    reduce_scatter x1, waiting for transfers between devices, shards(): lax.psum_scatter(running_sums[0], 'ctx', scatter_dimension=0, tiled=True)  70.6 us
    add x30, other arithmetic, reverse_merge(): later[1] + later[0][..., None, None] * earlier[1]  35.7 us
    psum x1, waiting for transfers between devices, shards(): running_sums = lax.psum((grad_qkv, grad_out, grad_embed), 'mix')  28.1 us
    all_gather x1, blocking collectives, prefix(): gathered = jax.tree.map(lambda a: lax.all_gather(a, axis), part)  26.6 us
    dot_general x12, matrix products, product(): return jnp.einsum(spec, left, right, preferred_element_type=jnp.float32)  18.1 us
  transfers between devices with their start and end apart: 6, of which 6 were waited for; matrix products, arithmetic and copies ran while one was open for 3% of the time, Pallas kernels for 0%

commit v1 on v0

v1 whole, which is shorter than its diff:
```python
import jax
import jax.numpy as jnp
from jax import lax
from jax.sharding import PartitionSpec as P

EPS = 1e-06
BF = jnp.bfloat16
F32 = jnp.float32


def mm(left, right, dims):
    return lax.dot_general(left.astype(BF), right.astype(BF), (dims, ((), ())), preferred_element_type=F32)


def shards(
    sources, source_ids, mix_weights, source_lengths, w_embed, w_qkv, w_out, forget, cotangent
):
    mix_index = lax.axis_index("mix")
    ctx_index = lax.axis_index("ctx")
    patch = w_embed.shape[1]
    local_sources = sources.shape[0]
    steps = sources.shape[1] // patch
    local_mix, heads = forget.shape[0], forget.shape[1]
    width = w_out.shape[0]
    head = width // heads
    lanes = heads * patch
    positions = ctx_index * steps + jnp.arange(steps, dtype=jnp.int32)
    own = mix_index * local_sources + jnp.arange(local_sources, dtype=jnp.int32)
    series = sources.reshape(local_sources, steps, patch)
    cover = jnp.where(positions[None, None, :] < source_lengths[:, :, None], mix_weights[:, :, None], 0.0)
    part = 0.0
    for s in range(local_sources):
        amount = jnp.sum(jnp.where((source_ids == own[s])[:, :, None], cover, 0.0), axis=1)
        part = part + amount[:, :, None] * series[s][None]
    mixture = lax.optimization_barrier(
        lax.psum_scatter(part, "mix", scatter_dimension=0, tiled=True)
    )
    m = mixture.astype(BF)

    wt = mm(w_embed, w_qkv, ((0,), (0,)))
    stack = lambda j: wt[:, j * width : (j + 1) * width].reshape(patch, heads, head).transpose(1, 0, 2).astype(BF)
    at, bt, ct = stack(0), stack(1), stack(2)
    gram = jnp.einsum("hid,hjd->hij", at, bt, preferred_element_type=F32).astype(BF)
    wo = jnp.einsum("hid,hdo->hio", ct, w_out.reshape(heads, head, width), preferred_element_type=F32).astype(BF)
    kk = jnp.einsum("hid,hjd->hij", ct, ct, preferred_element_type=F32).astype(BF)

    log_gate = jnp.log1p(forget - 1.0)
    g = jnp.cumsum(log_gate, axis=-1)
    last = g[..., -1:]
    causal = jnp.arange(steps)[:, None] >= jnp.arange(steps)[None, :]
    decay = jnp.where(causal, jnp.exp(g[..., :, None] - g[..., None, :]), 0.0)
    me = (m.astype(F32)[:, None] * jnp.exp(last - g)[..., None]).astype(BF)
    local = jnp.einsum("bti,bhtj->bhij", m, me, preferred_element_type=F32)
    packed = jnp.concatenate([local.reshape(-1), last.reshape(-1)])
    gathered = lax.all_gather(packed, "ctx")
    count = gathered.shape[0]
    ends = gathered[:, : local.size].reshape((count,) + local.shape)
    lasts = gathered[:, local.size :].reshape(count, local_mix, heads)
    before = jnp.cumsum(lasts, axis=0) - 0.0
    mine = lax.dynamic_index_in_dim(before - lasts, ctx_index, 0, True)
    earlier = (jnp.arange(count) < ctx_index)[:, None, None]
    factor = jnp.where(earlier, jnp.exp(jnp.where(earlier, mine - before, 0.0)), 0.0)
    memory = jnp.sum(factor[..., None, None] * ends, axis=0).astype(BF)

    mg = jnp.einsum("bti,hij->bhtj", m, gram, preferred_element_type=F32).astype(BF)
    scores = (jnp.einsum("bhtj,bsj->bhts", mg, m, preferred_element_type=F32) * decay).astype(BF)
    growth = jnp.exp(g)[..., None]
    mge = (mg.astype(F32) * growth).astype(BF)
    u = jnp.einsum("bhts,bsi->bhti", scores, m, preferred_element_type=F32) + jnp.einsum(
        "bhtj,bhji->bhti", mge, memory, preferred_element_type=F32
    )
    uh = u.astype(BF)
    read = jnp.einsum("bhti,hid->bhtd", uh, ct, preferred_element_type=F32)
    inv = lax.rsqrt(jnp.mean(read * read, axis=-1, keepdims=True) + EPS)
    n = (u * inv).astype(BF)
    output = jnp.einsum("bhti,hio->bto", n, wo, preferred_element_type=F32).astype(BF)
    y0 = jnp.einsum("bto,hio->bhti", cotangent, wo, preferred_element_type=F32)
    ku = jnp.einsum("bhti,hij->bhtj", uh, kk, preferred_element_type=F32)
    mu = inv * jnp.sum(y0 * u, axis=-1, keepdims=True) / head
    y = inv * (y0 - inv * mu * ku)
    yh = y.astype(BF)
    left = (jnp.einsum("bhtj,bsj->bhts", yh, m, preferred_element_type=F32) * decay).astype(BF)
    a = jnp.einsum("bhts,bsi->bhti", left, m, preferred_element_type=F32) + jnp.einsum(
        "bhtj,bhji->bhti", (y * growth).astype(BF), memory, preferred_element_type=F32
    )
    x = jnp.einsum("bti,bhtj->hij", m, a.astype(BF), preferred_element_type=F32)
    z = jnp.einsum("bhti,bto->hio", n, cotangent, preferred_element_type=F32)
    v = jnp.einsum("bhti,bhtj->hij", (u * inv * mu).astype(BF), n, preferred_element_type=F32)
    x, z, v = lax.optimization_barrier(lax.psum((x, z, v), ("ctx", "mix")))
    exact = lambda spec, left, right: jnp.einsum(
        spec, left, right.astype(F32), precision=lax.Precision.HIGHEST, preferred_element_type=F32
    )
    yq = exact("hij,hjd->hid", x, bt)
    yk = exact("hji,hjd->hid", x, at)
    yv = exact("hio,hdo->hid", z, w_out.reshape(heads, head, width)) - exact("hij,hjd->hid", v, ct)
    ys = jnp.concatenate([q.transpose(1, 0, 2).reshape(patch, width) for q in (yq, yk, yv)], axis=1)
    rows = width // count
    we = lax.dynamic_slice_in_dim(w_embed, ctx_index * rows, rows, 0)
    wq = lax.dynamic_slice_in_dim(w_qkv, ctx_index * rows, rows, 0)
    grad_qkv = mm(we, ys, ((1,), (0,)))
    grad_embed = mm(wq, ys, ((1,), (1,)))
    full = exact("hio,hid->hdo", z, ct).reshape(width, width)
    grad_out = lax.dynamic_slice_in_dim(full, ctx_index * rows, rows, 0)
    return (output, grad_qkv, grad_out, grad_embed)


def solution(mesh):
    placed = (
        P("mix", "ctx"),
        P(),
        P(),
        P(),
        P(),
        P(),
        P(),
        P("mix", None, "ctx"),
        P("mix", "ctx", None),
    )
    return jax.shard_map(
        shards,
        mesh=mesh,
        in_specs=placed,
        out_specs=(P("mix", "ctx", None), P("ctx", None), P("ctx", None), P("ctx", None)),
        check_vma=False,
    )
```

time: 572 us -> 319 us (0.56)
  waiting for transfers between devices: 406 us -> 192 us
  other arithmetic: 42.1 us -> 10.8 us
  matrix products: 30.2 us -> 16.2 us
  blocking collectives: 55.3 us -> 67 us
    reduce_scatter x3 -> x1, waiting for transfers between devices: 228 us -> 15.6 us  [shards(): lax.psum_scatter(part, 'mix', scatter_dimension=0, tiled=True)]
    all_gather x2 -> x0, waiting for transfers between devices: 150 us -> none  [prefix(): gathered = jax.tree.map(lambda a: lax.all_gather(a, axis), part)]
    unnamed x6 -> x4, waiting for transfers between devices: 0.1 us -> 105 us
    psum x1, blocking collectives: 15.1 us -> 67 us  [shards(): x, z, v = lax.optimization_barrier(lax.psum((x, z, v), ('ctx', 'mix')))]
    psum x1, waiting for transfers between devices: 28.1 us -> 71.4 us  [shards(): x, z, v = lax.optimization_barrier(lax.psum((x, z, v), ('ctx', 'mix')))]
    all_gather x2 -> x0, blocking collectives: 40.1 us -> none  [the longest x1 26.6 us: prefix(): gathered = jax.tree.map(lambda a: lax.all_gather(a, axis), part)]
    add x32 -> x3, other arithmetic: 36.9 us -> 0.78 us  [the longest x1 0.77 us: shards(): part = part + amount[:, :, None] * series[s][None]]
    dot_general x19 -> x23, matrix products: 30.2 us -> 16.2 us  [the longest x5 3.67 us: shards(): jnp.einsum(spec, left, right.astype(F32), precision=lax.Precision.HIGHEST...]
  transfers between devices with their start and end apart: 6 -> 3, of which waited for: 6 -> 3; matrix products, arithmetic and copies ran while one was open for 3% -> 4% of each run, Pallas kernels for 0% -> 0%
where the time goes in v1:
time: 319 us; the launch traced here: 318 us
  waiting for transfers between devices  192 us (60%)
  blocking collectives  67 us (21%)
  local copies, waits for them, and re-layouts  16.7 us (5%)
  matrix products  16.2 us (5%)
  between operations  15 us (5%)
  other arithmetic  10.8 us (3%)
    unnamed x4, waiting for transfers between devices  105 us
    psum x1, waiting for transfers between devices, shards(): x, z, v = lax.optimization_barrier(lax.psum((x, z, v), ('ctx', 'mix')))  71.4 us
    psum x1, blocking collectives, shards(): x, z, v = lax.optimization_barrier(lax.psum((x, z, v), ('ctx', 'mix')))  67 us
    reduce_scatter x1, waiting for transfers between devices, shards(): lax.psum_scatter(part, 'mix', scatter_dimension=0, tiled=True)  15.6 us
    mul x2, local copies, waits for them, and re-layouts, shards(): memory = jnp.sum(factor[..., None, None] * ends, axis=0).astype(BF)  6.59 us
  transfers between devices with their start and end apart: 3, of which 3 were waited for; matrix products, arithmetic and copies ran while one was open for 4% of the time, Pallas kernels for 0%

profile of v1, /device:TPU:1, one launch (start us, length us, event | category | flops | bytes accessed | tf_op | source)
XLA Modules:
  0.0 318.0 jit_solution(14915425428958048478)
XLA Ops:
  7.3 0.6 fusion.71
  7.9 1.6 slice_reduce_fusion.3
  10.1 3.3 %broadcast_compare_fusion.2 = (pred[8,3]{0,1:T(4,128)(4,1)S(1)}, pred[8,3]{0,1:T(4,128)(4,1)S(1)}, pred[8,3]{0,1:T(4,128)(4,1)S(1)}, pred[8,3]{0,1:T(4,128)(4,1)S(1)}) fusion(s32[8,3]{0,1:T(4,128)} %param.10, s32[]{:T(128)} %bitcast.4, s32[]{:T(128)} %bitcast.3, s32[]{:T(128)} %bitcast.6, s32[]{:T(128)} %bitcast.5), kind=kLoop, calls=%fused_computation.124 | loop fusion | flops 96 | bytes 208 | tf_op jit(solution)/shard_map/eq | solution.py:33
  13.4 0.8 fusion.53
  14.2 0.8 multiply_add_fusion
  15.1 2.4 reduce-window.6
  18.7 0.6 copy.167
  19.3 0.6 dynamic-slice
  20.7 0.8 fusion.6
  21.5 15.6 %reduce-scatter.2.cloned.1.call-done = f32[2,256,32]{1,2,0:T(8,128)} async-done(((f32[8,256,32]{1,2,0:T(8,128)}), f32[2,256,32]{1,2,0:T(8,128)}) %reduce-scatter.2.cloned.1.call-update) | async-done | bytes 65552 | tf_op jit(solution)/shard_map/reduce_scatter | solution.py:36
  37.2 0.8 fusion.70
  38.7 1.0 copy-done.1
  40.1 0.6 copy-done.6
  40.8 0.7 multiply_convert_fusion.1
  41.9 105.2 %all-reduce.7.cloned.1.call-done = f32[262400]{0:T(1024)} async-done(((f32[262400]{0:T(1024)}), f32[262400]{0:T(1024)}) %all-reduce.7.cloned.1.call-update) | async-done | bytes 1049616
  147.1 1.9 reshape.161
  149.3 2.3 mul.199
  151.6 4.3 %mul.200 = f32[32,8192]{1,0:T(8,128)} reshape(f32[32,2,4,32,32]{4,3,2,1,0:T(8,128)} %mul.199) | data formatting | bytes 2097152 | tf_op jit(solution)/shard_map/mul | solution.py:63
  155.9 2.0 fusion.16
  158.0 0.8 convert_element_type.105
  158.8 1.1 convolution_add_fusion.1
  160.4 0.9 convolution_bitcast_fusion.1
  161.7 0.8 convolution_bitcast_fusion.5
  162.9 0.7 multiply_convert_fusion
  164.4 67.0 %all-reduce.1 = (f32[4,32,32]{1,2,0:T(8,128)S(1)}, f32[4,32,32]{2,1,0:T(8,128)S(1)}) all-reduce(f32[4,32,32]{1,2,0:T(8,128)S(1)} %fusion.9, f32[4,32,32]{2,1,0:T(8,128)} %convolution_bitcast_fusion.5), channel_id=1, replica_groups=mesh['ctx'=32,'mix'=4] {'ctx','mix'}, use_global_device_ids=true, to_apply=%region_11.12 | all-reduce | flops 8192 | bytes 65536 | tf_op jit(solution)/shard_map/psum | solution.py:89
  231.4 2.0 fusion
  233.4 71.4 %all-reduce.5.cloned.1.call-done = f32[4,32,512]{2,1,0:T(8,128)} async-done(((f32[4,32,512]{2,1,0:T(8,128)}), f32[4,32,512]{2,1,0:T(8,128)}) %all-reduce.5.cloned.1.call-update) | async-done | bytes 262160 | tf_op jit(solution)/shard_map/psum | solution.py:89
  304.8 1.6 fusion.39
  306.4 1.5 fusion.74
  308.6 1.6 fusion.63
  310.1 0.7 fusion.37
  310.9 0.6 constant_dynamic-slice_fusion.1
  (98 shorter events, 6.2 us)
Async XLA Ops:
  7.2 11.1 %copy-start = (bf16[512,1536]{1,0:T(8,128)(2,1)S(1)}, bf16[512,1536]{1,0:T(8,128)(2,1)}, u32[]{:S(2)}) copy-start(bf16[512,1536]{1,0:T(8,128)(2,1)} %param.14) | copy-start | bytes 4718596
  7.2 7.9 %copy-start.19 = (f32[2,4,256]{2,1,0:T(4,128)S(1)}, f32[2,4,256]{2,1,0:T(4,128)}, u32[]{:S(2)}) copy-start(f32[2,4,256]{2,1,0:T(4,128)} %param.16) | copy-start | bytes 24580
  7.2 11.1 %copy-start.18 = (bf16[512,32]{0,1:T(8,128)(2,1)S(1)}, bf16[512,32]{0,1:T(8,128)(2,1)}, u32[]{:S(2)}) copy-start(bf16[512,32]{0,1:T(8,128)(2,1)} %param.13) | copy-start | bytes 98308
  7.2 29.9 %reduce-scatter.2.cloned.1.call-start = ((), (), s32[]{:S(2)}) async-start(), calls=%async_computation.1 | async-start | bytes 327680 | tf_op jit(solution)/shard_map/reduce_scatter | solution.py:36
  7.9 11.5 %copy-start.20 = (u32[128]{0:T(128)S(1)}, u32[128]{0:T(128)}, u32[]{:S(2)}) copy-start(u32[128]{0:T(128)} %constant.45) | copy-start | bytes 1540
  9.5 11.2 %copy-start.3 = (bf16[512,512]{1,0:T(8,128)(2,1)S(1)}, bf16[512,512]{1,0:T(8,128)(2,1)}, u32[]{:S(2)}) copy-start(bf16[512,512]{1,0:T(8,128)(2,1)} %param.15) | copy-start | bytes 1572868
  15.0 132.1 %all-reduce.7.cloned.1.call-start = ((), (), s32[]{:S(2)}) async-start(), calls=%async_computation.3 | async-start | bytes 2105344
  18.0 22.1 %copy-start.16 = (f32[2,4,256]{2,1,0:T(4,128)}, f32[2,4,256]{2,1,0:T(4,128)S(1)}, u32[]{:S(2)}) copy-start(f32[2,4,256]{2,1,0:T(4,128)S(1)} %reduce_window_sum.41) | copy-start | bytes 24580
  20.6 20.9 %copy-start.14 = (pred[256,256]{1,0:T(8,128)(4,1)}, pred[256,256]{1,0:T(8,128)(4,1)S(1)}, u32[]{:S(2)}) copy-start(pred[256,256]{1,0:T(8,128)(4,1)S(1)} %iota_compare_fusion) | copy-start | bytes 196612
  20.6 20.9 %copy-start.7 = (bf16[4,4,8,128]{3,2,1,0:T(8,128)(2,1)}, bf16[4,4,8,128]{3,2,1,0:T(8,128)(2,1)S(1)}, u32[]{:S(2)}) copy-start(bf16[4,4,8,128]{3,2,1,0:T(8,128)(2,1)S(1)} %get-tuple-element.24) | copy-start | bytes 98308
  20.6 20.9 %copy-start.9 = (bf16[4,4,8,128]{3,2,1,0:T(8,128)(2,1)}, bf16[4,4,8,128]{3,2,1,0:T(8,128)(2,1)S(1)}, u32[]{:S(2)}) copy-start(bf16[4,4,8,128]{3,2,1,0:T(8,128)(2,1)S(1)} %get-tuple-element.22) | copy-start | bytes 98308
  38.7 1.0 copy-start.1
  39.7 265.0 %all-reduce.5.cloned.1.call-start = ((), (), s32[]{:S(2)}) async-start(), calls=%async_computation.2 | async-start | bytes 524288 | tf_op jit(solution)/shard_map/psum | solution.py:89
  40.1 0.7 copy-start.6
  155.9 4.4 %copy-start.2 = (bf16[2,256,512]{2,1,0:T(8,128)(2,1)S(1)}, bf16[2,256,512]{2,1,0:T(8,128)(2,1)}, u32[]{:S(2)}) copy-start(bf16[2,256,512]{2,1,0:T(8,128)(2,1)} %param.17) | copy-start | bytes 1572868
  158.0 3.4 %copy-start.5 = (bf16[4,32,512,1]{2,1,3,0:T(8,128)(2,1)S(1)}, bf16[4,32,512,1]{2,1,3,0:T(8,128)(2,1)}, u32[]{:S(2)}) copy-start(bf16[4,32,512,1]{2,1,3,0:T(8,128)(2,1)} %fusion.6) | copy-start | bytes 393220
  160.3 2.6 copy-start.15
  160.3 2.5 copy-start.17
  160.4 2.5 copy-start.11
  162.9 1.1 copy-start.13
  163.6 67.8 %copy-start.12 = (f32[2,4,256]{2,0,1:T(2,128)S(1)}, f32[2,4,256]{2,0,1:T(2,128)}, u32[]{:S(2)}) copy-start(f32[2,4,256]{2,0,1:T(2,128)} %copy-done.11) | copy-start | bytes 24580
  164.0 142.3 %copy-start.4 = (bf16[512,512]{1,0:T(8,128)(2,1)S(1)}, bf16[512,512]{1,0:T(8,128)(2,1)}, u32[]{:S(2)}) copy-start(bf16[512,512]{1,0:T(8,128)(2,1)} %param.15) | copy-start | bytes 1572868
  164.0 143.9 %copy-start.10 = (bf16[4,4,8,128]{3,2,1,0:T(8,128)(2,1)S(1)}, bf16[4,4,8,128]{3,2,1,0:T(8,128)(2,1)}, u32[]{:S(2)}) copy-start(bf16[4,4,8,128]{3,2,1,0:T(8,128)(2,1)} %copy-done.9) | copy-start | bytes 98308
  164.4 143.7 %copy-start.8 = (bf16[4,4,8,128]{3,2,1,0:T(8,128)(2,1)S(1)}, bf16[4,4,8,128]{3,2,1,0:T(8,128)(2,1)}, u32[]{:S(2)}) copy-start(bf16[4,4,8,128]{3,2,1,0:T(8,128)(2,1)} %copy-done.7) | copy-start | bytes 98308
Sparse Core Ops, SparseCore 0:
  15.1 21.9 reduce-scatter.1
  40.5 106.5 all-reduce.6
  161.5 143.2 all-reduce.4

commit v2 on v1

v2 whole, which is shorter than its diff:
```python
import jax
import jax.numpy as jnp
from jax import lax
from jax.experimental import pallas as pl
from jax.experimental.pallas import tpu as pltpu
from jax.sharding import PartitionSpec as P

EPS = 1e-06
BF = jnp.bfloat16
F32 = jnp.float32
MESH = pl.DeviceIdType.MESH
NCTX = 32
NMIX = 4
NDEV = 128
LB = 2
HEADS = 4
PATCH = 32
STEPS = 256
ROWS = LB * STEPS
HEAD = 128
WIDTH = 512
LOCAL_SOURCES = 4
TERMS = 3
VX = WIDTH + HEAD


def mm(left, right, dims=((1,), (0,))):
    return lax.dot_general(left, right, (dims, ((), ())), preferred_element_type=F32)


NT = ((1,), (1,))
TN = ((0,), (0,))


def mm_exact(left, right, dims):
    return lax.dot_general(
        left, right, (dims, ((), ())), precision=lax.Precision.HIGHEST, preferred_element_type=F32
    )


def iota(shape, axis):
    return lax.broadcasted_iota(jnp.int32, shape, axis)


def kernel(
    src_hbm, ids_hbm, wts_hbm, lens_hbm, we_hbm, wq_hbm, wo_hbm, forget_hbm, cot_hbm,
    out_hbm, gqkv_hbm, gout_hbm, gemb_hbm,
    src, ids, wts, lens, we, wq, wo, forget, cot,
    stage_mix, recv_mix, glast, recv_g, m_local, recv_m, stage_s, recv_s,
    decay, m4, mgs, u_ref, a_ref, y_ref, gcol, at, bt, ct, ctbig, gram, kk, wop, y0,
    zall, recv_z, zrow, recv_zh, yxrow, recv_yx,
    out, gqkv, gout, gemb, spare_g, spare_m, spare_s, spare_z, spare_yx, spare_zh,
    in_sem, mix_s, mix_r, g_s, g_r, m_s, m_r, s_s, s_r, z_s, z_r, zh_s, zh_r, yx_s, yx_r, out_sem,
):
    ctx = lax.axis_index("ctx")
    mix = lax.axis_index("mix")
    me = ctx * NMIX + mix
    plane = ctx // 8

    moves = [
        (ids_hbm, ids), (wts_hbm, wts), (lens_hbm, lens), (forget_hbm, forget),
        (we_hbm, we), (wq_hbm, wq), (wo_hbm, wo), (cot_hbm, cot),
    ] + [(src_hbm.at[:, s], src.at[s]) for s in range(LOCAL_SOURCES)]
    loads = [pltpu.make_async_copy(a, b, in_sem.at[i]) for i, (a, b) in enumerate(moves)]
    for i in (8, 9, 10, 11, 0, 1, 2, 3, 4, 5, 6, 7):
        loads[i].start()

    def device(flat):
        return (flat // NMIX, lax.rem(flat, NMIX))

    barrier = pltpu.get_barrier_semaphore()

    def greet(o, carry):
        pl.semaphore_signal(
            barrier, inc=1, device_id=device(lax.rem(me + o, NDEV)), device_id_type=MESH
        )
        return carry

    lax.fori_loop(1, NDEV, greet, 0)

    for load in loads[:3] + loads[8:]:
        load.wait()
    place = ctx * STEPS + 4 * iota((64, 128), 0) + iota((64, 128), 1) // PATCH
    for b in range(LB * NMIX):
        part = jnp.zeros((64, 128), F32)
        for j in range(TERMS):
            slot = ids[j, b] - mix * LOCAL_SOURCES
            held = jnp.clip(slot, 0, LOCAL_SOURCES - 1)
            weight = jnp.where(slot == held, wts[j, b], 0.0)
            part = part + jnp.where(place < lens[j, b], weight, 0.0) * src[held]
        stage_mix[b] = part

    loads[3].wait()
    tri = (iota((STEPS, STEPS), 0) >= iota((STEPS, STEPS), 1)).astype(F32)
    growth = []
    for b in range(LB):
        gate = jnp.log1p(forget[b] - 1.0)
        wide = jnp.concatenate(
            [jnp.broadcast_to(gate[h : h + 1], (PATCH, STEPS)) for h in range(HEADS)], axis=0
        )
        col = mm_exact(tri, wide, NT)
        gcol[b] = col
        glast[b : b + 1] = col[STEPS - 1 : STEPS]
        growth.append(mm_exact(gate, tri, NT))

    pl.semaphore_wait(barrier, NDEV - 1)

    own_mix = pltpu.make_async_copy(stage_mix.at[pl.ds(LB * mix, LB)], recv_mix.at[mix], mix_r)
    own_mix.start()
    for o in range(1, NMIX):
        other = lax.rem(mix + o, NMIX)
        pltpu.make_async_remote_copy(
            stage_mix.at[pl.ds(LB * other, LB)], recv_mix.at[mix], mix_s, mix_r,
            device_id=(ctx, other), device_id_type=MESH,
        ).start()

    def spare_copy(part, spare, send):
        pltpu.make_async_copy(part, spare, send).start()

    def ctx_rows(spare, src_ref, dst_ref, send, recv, src_row, dst_row):
        def one(o, carry):
            other = lax.rem(ctx + o, NCTX)
            pltpu.make_async_remote_copy(
                src_ref.at[pl.ds(src_row(other), 2)], dst_ref.at[pl.ds(dst_row, 2)], send, recv,
                device_id=(other, mix), device_id_type=MESH,
            ).start()
            return carry

        lax.fori_loop(1, NCTX, one, 0)
        spare_copy(src_ref.at[pl.ds(src_row(ctx), 2)], spare, send)
        pltpu.make_async_copy(
            src_ref.at[pl.ds(src_row(ctx), 2)], dst_ref.at[pl.ds(dst_row, 2)], recv
        ).start()

    ctx_rows(spare_g, glast, recv_g, g_s, g_r, lambda other: 0, 2 * ctx)

    for load in loads[4:7]:
        load.wait()
    wt = mm(we[...], wq[...]).astype(BF)
    lane = iota((1, HEAD), 1)
    block = iota((HEAD, HEAD), 0) // PATCH == iota((HEAD, HEAD), 1) // PATCH
    heads = [lane // PATCH == h for h in range(HEADS)]
    for h in range(HEADS):
        rows = pl.ds(h * PATCH, PATCH)
        at[rows] = wt[:, h * HEAD : (h + 1) * HEAD]
        bt[rows] = wt[:, WIDTH + h * HEAD : WIDTH + (h + 1) * HEAD]
        piece = wt[:, 2 * WIDTH + h * HEAD : 2 * WIDTH + (h + 1) * HEAD]
        ct[rows] = piece
        for k in range(HEADS):
            ctbig[rows, k * HEAD : (k + 1) * HEAD] = piece if k == h else jnp.zeros_like(piece)
    gram[...] = jnp.where(block, mm(at[...], bt[...], NT), 0.0).astype(BF)
    kk[...] = jnp.where(block, mm(ct[...], ct[...], NT), 0.0).astype(BF)
    wop[...] = mm(ctbig[...], wo[...]).astype(BF)
    loads[7].wait()
    y0[...] = mm(cot[...], wop[...], NT)

    causal = iota((STEPS, STEPS), 0) >= iota((STEPS, STEPS), 1)
    for b in range(LB):
        for h in range(HEADS):
            diff = gcol[b][:, h * PATCH : h * PATCH + 1] - growth[b][h : h + 1]
            decay[b * HEADS + h] = jnp.where(causal, jnp.exp(diff), 0.0)

    pltpu.make_async_copy(recv_mix, recv_mix, mix_r).wait()
    spread = (lax.rem(iota((HEAD, HEAD), 0), PATCH) == lax.rem(iota((HEAD, HEAD), 1), PATCH)).astype(BF)
    pick = (iota((STEPS, 64), 0) // 4 == iota((STEPS, 64), 1)).astype(BF)
    mine = lax.rem(iota((STEPS, HEAD), 0), 4) == iota((STEPS, HEAD), 1) // PATCH
    for b in range(LB):
        packed = ((recv_mix[0, b] + recv_mix[1, b]) + (recv_mix[2, b] + recv_mix[3, b])).astype(BF)
        lone = jnp.where(mine, mm(pick, packed), 0.0).astype(BF)
        rows = mm(lone, spread)
        m4[pl.ds(b * STEPS, STEPS)] = rows.astype(BF)
        faded = (rows * jnp.exp(glast[b : b + 1] - gcol[b])).astype(BF)
        m_local[pl.ds(b * PATCH, PATCH)] = mm(rows.astype(BF), faded, TN)[:PATCH]
    ctx_rows(spare_m, m_local, recv_m, m_s, m_r, lambda other: 2 * other, 2 * ctx)

    for b in range(LB):
        rows = pl.ds(b * STEPS, STEPS)
        mb = m4[rows]
        mg = mm(mb, gram[...])
        mgs[rows] = (mg * jnp.exp(gcol[b])).astype(BF)
        mgb = mg.astype(BF)
        total = jnp.zeros((STEPS, HEAD), F32)
        for h in range(HEADS):
            score = mm(jnp.where(heads[h], mgb, jnp.zeros_like(mgb)), mb, NT)
            score = (score * decay[b * HEADS + h]).astype(BF)
            total = total + mm(score, jnp.where(heads[h], mb, jnp.zeros_like(mb)))
        u_ref[rows] = total

    pltpu.make_async_copy(recv_g, recv_g, g_r).wait()
    pltpu.make_async_copy(recv_m, recv_m, m_r).wait()
    own_b = ctx // (NCTX // LB)
    state = jnp.zeros((2, HEAD), F32)
    for j in range(NCTX):
        stage_s[2 * j : 2 * j + 2] = state
        state = jnp.exp(recv_g[pl.ds(2 * j + own_b, 1)]) * state + recv_m[2 * j : 2 * j + 2]
    ctx_rows(spare_s, stage_s, recv_s, s_s, s_r, lambda other: 2 * other, 2 * ctx)
    pltpu.make_async_copy(recv_s, recv_s, s_r).wait()

    memory = []
    for b in range(LB):
        part = recv_s[pl.ds(b * PATCH, PATCH)]
        memory.append(
            jnp.where(block, jnp.concatenate([part] * HEADS, axis=0), 0.0).astype(BF)
        )
        rows = pl.ds(b * STEPS, STEPS)
        u_ref[rows] = u_ref[rows] + mm(mgs[rows], memory[b])
    u = u_ref[...]
    ub = u.astype(BF)
    read = mm(ub, ctbig[...])
    sums = (iota((WIDTH, HEAD), 0) // HEAD == iota((WIDTH, HEAD), 1) // PATCH).astype(BF)
    square = mm((read * read).astype(BF), sums) * (1.0 / HEAD)
    inv = lax.rsqrt(square + EPS)
    n = u * inv
    nb = n.astype(BF)
    dots = mm((y0[...] * u).astype(BF), block.astype(BF)) * (1.0 / HEAD)
    drift = inv * (inv * dots)
    y = inv * (y0[...] - drift * mm(ub, kk[...]))
    y_ref[...] = y
    for b in range(LB):
        rows = pl.ds(b * STEPS, STEPS)
        mb = m4[rows]
        yb = y_ref[rows]
        yh = yb.astype(BF)
        total = mm((yb * jnp.exp(gcol[b])).astype(BF), memory[b])
        for h in range(HEADS):
            left = mm(jnp.where(heads[h], yh, jnp.zeros_like(yh)), mb, NT)
            left = (left * decay[b * HEADS + h]).astype(BF)
            total = total + mm(left, jnp.where(heads[h], mb, jnp.zeros_like(mb)))
        a_ref[rows] = total.astype(BF)

    def repeat(square_block):
        kept = jnp.where(block, square_block, 0.0)
        kept = kept + pltpu.roll(kept, 64, 1)
        return kept + pltpu.roll(kept, 32, 1)

    zall[:, :WIDTH] = mm(nb, cot[...], TN)
    v_rows = repeat(mm((n * (inv * dots)).astype(BF), nb, TN))
    x_rows = repeat(mm(m4[...], a_ref[...], TN))
    zall[:, WIDTH:] = jnp.where(lane < 64, v_rows, x_rows)

    def scatter(o, carry):
        other = lax.rem(me + o, NDEV)
        pltpu.make_async_remote_copy(
            zall.at[pl.ds(other, 1)], recv_z.at[pl.ds(me, 1)], z_s, z_r,
            device_id=device(other), device_id_type=MESH,
        ).start()
        return carry

    lax.fori_loop(1, NDEV, scatter, 0)
    spare_copy(zall.at[pl.ds(me, 1)], spare_z, z_s)
    pltpu.make_async_copy(zall.at[pl.ds(me, 1)], recv_z.at[pl.ds(me, 1)], z_r).start()

    out[...] = mm(nb, wop[...]).astype(BF)
    store_out = pltpu.make_async_copy(out, out_hbm, out_sem.at[0])
    store_out.start()

    pltpu.make_async_copy(recv_z, recv_z, z_r).wait()
    row = jnp.sum(recv_z[...], axis=0, keepdims=True)
    zrow[...] = row[:, :WIDTH]
    mixed = row[:, WIDTH:]
    fine = row[:, :WIDTH]
    high = fine.astype(BF)
    low = (fine - high.astype(F32)).astype(BF)
    w_head = wo[pl.ds(plane * HEAD, HEAD)]
    c_head = ct[pl.ds(plane * PATCH, PATCH)]
    yv = mm(high, w_head, NT) + mm(low, w_head, NT) - mm(mixed[:, :PATCH].astype(BF), c_head)
    xs = jnp.where(lane < 64, 0.0, mixed)
    yxrow[:, :HEAD] = yv
    yxrow[:, HEAD:] = xs + pltpu.roll(xs, 64, 1)

    def spread_row(o, carry):
        pltpu.make_async_remote_copy(
            yxrow, recv_yx.at[pl.ds(me, 1)], yx_s, yx_r,
            device_id=device(lax.rem(me + o, NDEV)), device_id_type=MESH,
        ).start()
        return carry

    lax.fori_loop(1, NDEV, spread_row, 0)
    spare_copy(yxrow, spare_yx, yx_s)
    pltpu.make_async_copy(yxrow, recv_yx.at[pl.ds(me, 1)], yx_r).start()
    local = lax.rem(me, NCTX)

    def spread_z(o, carry):
        pltpu.make_async_remote_copy(
            zrow, recv_zh.at[pl.ds(local, 1)], zh_s, zh_r,
            device_id=device(plane * NCTX + lax.rem(local + o, NCTX)), device_id_type=MESH,
        ).start()
        return carry

    lax.fori_loop(1, NCTX, spread_z, 0)
    spare_copy(zrow, spare_zh, zh_s)
    pltpu.make_async_copy(zrow, recv_zh.at[pl.ds(local, 1)], zh_r).start()

    chosen = (iota((16, HEAD), 1) == 16 * lax.rem(ctx, 8) + iota((16, HEAD), 0)).astype(BF)
    c_rows = mm(chosen, c_head, NT).astype(BF)
    column = (iota((16, WIDTH), 1) == ctx * 16 + iota((16, WIDTH), 0)).astype(BF)
    embed_rows = mm(column, jnp.concatenate([we[...]] * HEADS, axis=0), NT).astype(BF)
    tall = jnp.concatenate([jnp.where(heads[h], embed_rows, jnp.zeros_like(embed_rows)) for h in range(HEADS)], axis=0)
    qkv_rows = wq[pl.ds(ctx * 16, 16)]
    long = jnp.concatenate(
        [
            jnp.concatenate(
                [qkv_rows[:, j * WIDTH + h * HEAD : j * WIDTH + (h + 1) * HEAD] for j in range(3)], axis=1
            )
            for h in range(HEADS)
        ],
        axis=0,
    )

    pltpu.make_async_copy(recv_yx, recv_yx, yx_r).wait()
    x_block = jnp.where(block, recv_yx[:, HEAD:], 0.0).astype(BF)
    yq = mm(x_block, bt[...])
    yk = mm(x_block, at[...], TN)
    ys = jnp.concatenate([yq, yk, recv_yx[:, :HEAD]], axis=1).astype(BF)
    wide = mm(tall, ys)
    for h in range(HEADS):
        for j in range(3):
            gqkv[:, j * WIDTH + h * HEAD : j * WIDTH + (h + 1) * HEAD] = wide[
                16 * h : 16 * h + 16, j * HEAD : (j + 1) * HEAD
            ]
    tops = mm(long, ys, NT)
    folded = jnp.zeros((16, HEAD), F32)
    for h in range(HEADS):
        folded = folded + jnp.where(heads[h], tops[16 * h : 16 * h + 16], 0.0)
    folded = folded + pltpu.roll(folded, 64, 1)
    folded = folded + pltpu.roll(folded, 32, 1)
    gemb[...] = folded[:, :PATCH]
    store_qkv = pltpu.make_async_copy(gqkv, gqkv_hbm, out_sem.at[1])
    store_qkv.start()
    store_emb = pltpu.make_async_copy(gemb, gemb_hbm, out_sem.at[2])
    store_emb.start()
    pltpu.make_async_copy(recv_zh, recv_zh, zh_r).wait()
    gout[...] = mm(c_rows, recv_zh[...].astype(BF))
    store_gout = pltpu.make_async_copy(gout, gout_hbm, out_sem.at[3])
    store_gout.start()

    sent_mix = stage_mix.at[pl.ds(0, LB * (NMIX - 1))]
    pltpu.make_async_copy(sent_mix, sent_mix, mix_s).wait()
    for ref, sem in (
        (recv_g, g_s), (recv_m, m_s), (recv_s, s_s), (recv_z, z_s), (recv_yx, yx_s), (recv_zh, zh_s)
    ):
        pltpu.make_async_copy(ref, ref, sem).wait()
    for store in (store_out, store_qkv, store_emb, store_gout):
        store.wait()


def hand_on(*refs):
    source, target, held, (come, go) = refs[:4], refs[4:8], refs[8:12], refs[12:]
    pieces = [pl.ds(i * STEPS // 2, STEPS // 2) for i in range(2 * LB)]
    moves = [(source[0].at[p], held[0].at[p], target[0].at[p]) for p in pieces]
    moves += [(source[i], held[i], target[i]) for i in range(1, 4)]
    arrive = [pltpu.make_async_copy(a, b, come.at[i]) for i, (a, b, c) in enumerate(moves)]
    leave = [pltpu.make_async_copy(b, c, go.at[i]) for i, (a, b, c) in enumerate(moves)]
    for copy in arrive:
        copy.start()
    for copy, after in zip(arrive, leave):
        copy.wait()
        after.start()
    for copy in leave:
        copy.wait()


def shards(
    sources, source_ids, mix_weights, source_lengths, w_embed, w_qkv, w_out, forget, cotangent
):
    packed = sources.reshape(LOCAL_SOURCES, STEPS * PATCH // 128, 128).transpose(1, 0, 2)
    vm = pltpu.VMEM
    sm = pltpu.SMEM
    dma = pltpu.SemaphoreType.DMA
    results = pl.pallas_call(
        kernel,
        out_shape=(
            jax.ShapeDtypeStruct((ROWS, WIDTH), BF),
            jax.ShapeDtypeStruct((16, 3 * WIDTH), F32),
            jax.ShapeDtypeStruct((16, WIDTH), F32),
            jax.ShapeDtypeStruct((16, PATCH), F32),
        ),
        in_specs=[pl.BlockSpec(memory_space=pl.ANY)] * 9,
        out_specs=(pl.BlockSpec(memory_space=pl.ANY),) * 4,
        scratch_shapes=[
            vm((LOCAL_SOURCES, 64, 128), F32),
            sm((TERMS, LB * NMIX), jnp.int32),
            sm((TERMS, LB * NMIX), F32),
            sm((TERMS, LB * NMIX), jnp.int32),
            vm((PATCH, WIDTH), BF),
            vm((WIDTH, 3 * WIDTH), BF),
            vm((WIDTH, WIDTH), BF),
            vm((LB, HEADS, STEPS), F32),
            vm((ROWS, WIDTH), BF),
            vm((LB * NMIX, 64, 128), F32),
            vm((NMIX, LB, 64, 128), F32),
            vm((LB, HEAD), F32),
            vm((2 * NCTX, HEAD), F32),
            vm((2 * NCTX, HEAD), F32),
            vm((2 * NCTX, HEAD), F32),
            vm((2 * NCTX, HEAD), F32),
            vm((2 * NCTX, HEAD), F32),
            vm((LB * HEADS, STEPS, STEPS), F32),
            vm((ROWS, HEAD), BF),
            vm((ROWS, HEAD), BF),
            vm((ROWS, HEAD), F32),
            vm((ROWS, HEAD), BF),
            vm((ROWS, HEAD), F32),
            vm((LB, STEPS, HEAD), F32),
            vm((HEAD, HEAD), BF),
            vm((HEAD, HEAD), BF),
            vm((HEAD, HEAD), BF),
            vm((HEAD, WIDTH), BF),
            vm((HEAD, HEAD), BF),
            vm((HEAD, HEAD), BF),
            vm((HEAD, WIDTH), BF),
            vm((ROWS, HEAD), F32),
            vm((NDEV, VX), F32),
            vm((NDEV, VX), F32),
            vm((1, WIDTH), F32),
            vm((NCTX, WIDTH), F32),
            vm((1, 2 * HEAD), F32),
            vm((NDEV, 2 * HEAD), F32),
            vm((ROWS, WIDTH), BF),
            vm((16, 3 * WIDTH), F32),
            vm((16, WIDTH), F32),
            vm((16, PATCH), F32),
            vm((2, HEAD), F32),
            vm((2, HEAD), F32),
            vm((2, HEAD), F32),
            vm((1, VX), F32),
            vm((1, 2 * HEAD), F32),
            vm((1, WIDTH), F32),
            dma((12,)),
        ]
        + [dma(())] * 14
        + [dma((4,))],
        compiler_params=pltpu.CompilerParams(collective_id=0, has_side_effects=True, vmem_limit_bytes=60 << 20),
        name="whole_step",
    )(
        packed, source_ids.T, mix_weights.T, source_lengths.T, w_embed.T, w_qkv, w_out, forget,
        cotangent.reshape(ROWS, WIDTH),
    )
    output, grad_qkv, grad_out, grad_embed = pl.pallas_call(
        hand_on,
        out_shape=tuple(jax.ShapeDtypeStruct(r.shape, r.dtype) for r in results),
        in_specs=[pl.BlockSpec(memory_space=pl.ANY)] * 4,
        out_specs=(pl.BlockSpec(memory_space=pl.ANY),) * 4,
        scratch_shapes=[vm(r.shape, r.dtype) for r in results] + [dma((8,)), dma((8,))],
        name="hand_on",
    )(*results)
    return (output.reshape(LB, STEPS, WIDTH), grad_qkv, grad_out, grad_embed)


def solution(mesh):
    placed = (
        P("mix", "ctx"),
        P(),
        P(),
        P(),
        P(),
        P(),
        P(),
        P("mix", None, "ctx"),
        P("mix", "ctx", None),
    )
    return jax.shard_map(
        shards,
        mesh=mesh,
        in_specs=placed,
        out_specs=(P("mix", "ctx", None), P("ctx", None), P("ctx", None), P("ctx", None)),
        check_vma=False,
    )
```

time: 319 us -> 48.4 us (0.15)
  waiting for transfers between devices: 192 us -> 0 us
  blocking collectives: 67 us -> 0 us
  Pallas kernels: 0 us -> 47.7 us
  local copies, waits for them, and re-layouts: 16.7 us -> 0 us
  matrix products: 16.2 us -> 0 us
  between operations: 15 us -> 0.64 us
  other arithmetic: 10.8 us -> 0 us
    unnamed x4 -> x0, waiting for transfers between devices: 105 us -> none
    psum x1 -> x0, waiting for transfers between devices: 71.4 us -> none  [shards(): x, z, v = lax.optimization_barrier(lax.psum((x, z, v), ('ctx', 'mix')))]
    psum x1 -> x0, blocking collectives: 67 us -> none  [shards(): x, z, v = lax.optimization_barrier(lax.psum((x, z, v), ('ctx', 'mix')))]
    pallas_call x0 -> x2, Pallas kernels: none -> 47.7 us  [the longest x1 45.7 us: shards(): pl.pallas_call(kernel, out_shape=(jax.ShapeDtypeStruct((ROWS, WIDTH), BF)...]
    dot_general x23 -> x0, matrix products: 16.2 us -> none  [the longest x5 3.67 us: shards(): jnp.einsum(spec, left, right.astype(F32), precision=lax.Precision.HIGHEST...]
    reduce_scatter x1 -> x0, waiting for transfers between devices: 15.6 us -> none  [shards(): lax.psum_scatter(part, 'mix', scatter_dimension=0, tiled=True)]
    mul x10 -> x0, local copies, waits for them, and re-layouts: 7.24 us -> none  [the longest x2 6.59 us: shards(): memory = jnp.sum(factor[..., None, None] * ends, axis=0).astype(BF)]
    eq x1 -> x0, other arithmetic: 3.29 us -> none  [shards(): source_ids == own[s]]
  transfers between devices with their start and end apart: 3 -> 0, of which waited for: 3 -> 0; matrix products, arithmetic and copies ran while one was open for 4% -> 0% of each run, Pallas kernels for 0% -> 0%
where the time goes in v2:
time: 48.4 us; the launch traced here: 48.3 us
  Pallas kernels  47.7 us (99%)
  between operations  0.64 us (1%)
    pallas_call x1, Pallas kernels, shards(): pl.pallas_call(kernel, out_shape=(jax.ShapeDtypeStruct((ROWS, WIDTH), BF)...  45.7 us
    pallas_call x1, Pallas kernels, shards(): pl.pallas_call(hand_on, out_shape=tuple((jax.ShapeDtypeStruct(r.shape, r....  1.94 us

profile of v2, /device:TPU:1, one launch (start us, length us, event | category | flops | bytes accessed | tf_op | source)
XLA Modules:
  0.0 48.3 jit_solution(6055914771499043137)
XLA Ops:
  0.6 45.7 %whole_step.1 = (bf16[512,512]{1,0:T(8,128)(2,1)}, f32[16,1536]{1,0:T(8,128)}, f32[16,512]{1,0:T(8,128)}, f32[16,32]{1,0:T(8,128)}) custom-call(f32[64,4,128]{2,1,0:T(4,128)} %bitcast.10, s32[3,8]{1,0:T(4,128)} %bitcast.12, f32[3,8]{1,0:T(4,128)} %bitcast.13, s32[3,8]{1,0:T(4,128)} %bitcast.14, bf16[32,512]{1,0:T(8,128)(2,1)} %bitcast.11, ...), custom_call_target="tpu_custom_call" | custom-call | tf_op jit(solution)/shard_map/whole_step/pallas_call | solution.py:370
  46.4 1.9 %hand_on.1 = (bf16[512,512]{1,0:T(8,128)(2,1)}, f32[16,1536]{1,0:T(8,128)}, f32[16,512]{1,0:T(8,128)}, f32[16,32]{1,0:T(8,128)}) custom-call(bf16[512,512]{1,0:T(8,128)(2,1)} %get-tuple-element.12.refs_0_, f32[16,1536]{1,0:T(8,128)} %get-tuple-element.13.refs_1_, f32[16,512]{1,0:T(8,128)} %get-tuple-element.14.refs_2_, f32[16,32]{1,0:T(8,128)} %get-tuple-element.15.refs_3_), custom_call_target="tpu_custom_call" | custom-call | tf_op jit(solution)/shard_map/hand_on/pallas_call | solution.py:439

commit v3 on v2

v3 whole, which is shorter than its diff:
```python
import jax
import jax.numpy as jnp
from jax import lax
from jax.experimental import pallas as pl
from jax.experimental.pallas import tpu as pltpu
from jax.sharding import PartitionSpec as P

EPS = 1e-06
BF = jnp.bfloat16
F32 = jnp.float32
MESH = pl.DeviceIdType.MESH
NCTX = 32
NMIX = 4
NDEV = 128
LB = 2
HEADS = 4
PATCH = 32
STEPS = 256
ROWS = LB * STEPS
HEAD = 128
WIDTH = 512
LOCAL_SOURCES = 4
TERMS = 3
VX = WIDTH + HEAD
RESULTS = (((ROWS, WIDTH), BF), ((16, 3 * WIDTH), F32), ((16, WIDTH), F32), ((16, PATCH), F32))


def mm(left, right, dims=((1,), (0,))):
    return lax.dot_general(left, right, (dims, ((), ())), preferred_element_type=F32)


NT = ((1,), (1,))
TN = ((0,), (0,))


def mm_exact(left, right, dims):
    return lax.dot_general(
        left, right, (dims, ((), ())), precision=lax.Precision.HIGHEST, preferred_element_type=F32
    )


def far(d):
    return min(d, 4 - d)


CTX_STEPS = sorted(
    ((y, x, c) for y in range(4) for x in range(4) for c in range(2) if y or x or c),
    key=lambda o: -(3 * far(o[0]) + 3 * far(o[1]) + o[2]),
)
ALL_STEPS = sorted(
    ((y, x, c, z) for y in range(4) for x in range(4) for c in range(2) for z in range(4) if y or x or c or z),
    key=lambda o: -(3 * far(o[0]) + 3 * far(o[1]) + o[2] + 3 * far(o[3])),
)


def iota(shape, axis):
    return lax.broadcasted_iota(jnp.int32, shape, axis)


def kernel(
    src_hbm, ids_hbm, wts_hbm, lens_hbm, we_hbm, wq_hbm, wo_hbm, forget_hbm, cot_hbm,
    out, gqkv, gout, gemb,
    src, ids, wts, lens, we, wq, wo, forget, cot,
    stage_mix, recv_mix, glast, recv_g, m_local, recv_m, stage_s, recv_s,
    rise, fade, decay, m4, mgs, u_ref, a_ref, y_ref, gcol, at, bt, ct, ctbig, gram, kk, wop, y0,
    zall, recv_z, xall, recv_x, zrow, recv_zh, yxrow, recv_yx,
    spare_g, spare_m, spare_s, spare_z, spare_x, spare_yx, spare_zh,
    in_sem, mix_s, mix_r, g_s, g_r, m_s, m_r, s_s, s_r, z_s, z_r, x_s, x_r, zh_s, zh_r, yx_s, yx_r,
):
    ctx = lax.axis_index("ctx")
    mix = lax.axis_index("mix")
    me = ctx * NMIX + mix
    plane = ctx // 8

    moves = [
        (ids_hbm, ids), (wts_hbm, wts), (lens_hbm, lens),
        (we_hbm, we), (wq_hbm, wq), (wo_hbm, wo), (cot_hbm, cot),
    ]
    moves = [(src_hbm.at[:, s], src.at[s]) for s in range(LOCAL_SOURCES)] + moves
    moves += [(forget_hbm.at[b], forget.at[pl.ds(b * HEADS, HEADS)]) for b in range(LB)]
    copies = [pltpu.make_async_copy(a, b, in_sem.at[i]) for i, (a, b) in enumerate(moves)]
    part_loads, weight_loads, cot_load, gate_loads = copies[:7], copies[7:10], copies[10], copies[11:]
    for copy in part_loads + gate_loads + weight_loads + [cot_load]:
        copy.start()

    ys = [lax.rem(ctx // 8 + d, 4) * 8 for d in range(4)]
    xs = [lax.rem(ctx // 2 + d, 4) * 2 for d in range(4)]
    cs = [lax.rem(ctx + d, 2) for d in range(2)]
    zs = [lax.rem(mix + d, NMIX) for d in range(NMIX)]
    ctx_partners = [ys[y] + xs[x] + cs[c] for y, x, c in CTX_STEPS]
    all_partners = [(ys[y] + xs[x] + cs[c], zs[z]) for y, x, c, z in ALL_STEPS]
    plane_partners = [(ys[y] + xs[x] + cs[c], zs[z]) for y, x, c, z in ALL_STEPS if y == 0]

    barrier = pltpu.get_barrier_semaphore()
    for other in ctx_partners:
        pl.semaphore_signal(barrier, inc=1, device_id=(other, mix), device_id_type=MESH)
    for other in zs[1:]:
        pl.semaphore_signal(barrier, inc=1, device_id=(ctx, other), device_id_type=MESH)

    for load in part_loads:
        load.wait()
    place = ctx * STEPS + 4 * iota((64, 128), 0) + iota((64, 128), 1) // PATCH
    for b in range(LB * NMIX):
        part = jnp.zeros((64, 128), F32)
        for j in range(TERMS):
            slot = ids[j, b] - mix * LOCAL_SOURCES
            held = jnp.clip(slot, 0, LOCAL_SOURCES - 1)
            weight = jnp.where(slot == held, wts[j, b], 0.0)
            part = part + jnp.where(place < lens[j, b], weight, 0.0) * src[held]
        stage_mix[b] = part

    pl.semaphore_wait(barrier, NCTX - 1 + NMIX - 1)

    own_mix = pltpu.make_async_copy(stage_mix.at[pl.ds(LB * mix, LB)], recv_mix.at[mix], mix_r)
    own_mix.start()
    for other in (zs[2], zs[1], zs[3]):
        pltpu.make_async_remote_copy(
            stage_mix.at[pl.ds(LB * other, LB)], recv_mix.at[mix], mix_s, mix_r,
            device_id=(ctx, other), device_id_type=MESH,
        ).start()

    def spare_copy(part, spare, send):
        pltpu.make_async_copy(part, spare, send).start()

    def ctx_rows(spare, src_ref, dst_ref, send, recv, src_row, dst_row):
        for other in ctx_partners:
            pltpu.make_async_remote_copy(
                src_ref.at[pl.ds(src_row(other), 2)], dst_ref.at[pl.ds(dst_row, 2)], send, recv,
                device_id=(other, mix), device_id_type=MESH,
            ).start()
        spare_copy(src_ref.at[pl.ds(src_row(ctx), 2)], spare, send)
        pltpu.make_async_copy(
            src_ref.at[pl.ds(src_row(ctx), 2)], dst_ref.at[pl.ds(dst_row, 2)], recv
        ).start()

    for load in gate_loads:
        load.wait()
    growth = jnp.log1p(forget[...] - 1.0)
    lanes = iota((LB * HEADS, STEPS), 1)
    for k in (1, 2, 4, 8, 16, 32, 64, 128):
        growth = growth + jnp.where(lanes >= k, pltpu.roll(growth, k, 1), 0.0)
    for b in range(LB):
        col = jnp.concatenate(
            [
                jnp.broadcast_to(growth[b * HEADS + h : b * HEADS + h + 1], (PATCH, STEPS))
                for h in range(HEADS)
            ],
            axis=0,
        ).T
        gcol[b] = col
        last = col[STEPS - 1 : STEPS]
        glast[b : b + 1] = last
        rise[b] = jnp.exp(col)
        fade[b] = jnp.exp(last - col)

    ctx_rows(spare_g, glast, recv_g, g_s, g_r, lambda other: 0, 2 * ctx)

    for load in weight_loads:
        load.wait()
    wt = mm(we[...], wq[...]).astype(BF)
    lane = iota((1, HEAD), 1)
    block = iota((HEAD, HEAD), 0) // PATCH == iota((HEAD, HEAD), 1) // PATCH
    heads = [lane // PATCH == h for h in range(HEADS)]
    for h in range(HEADS):
        rows = pl.ds(h * PATCH, PATCH)
        at[rows] = wt[:, h * HEAD : (h + 1) * HEAD]
        bt[rows] = wt[:, WIDTH + h * HEAD : WIDTH + (h + 1) * HEAD]
        piece = wt[:, 2 * WIDTH + h * HEAD : 2 * WIDTH + (h + 1) * HEAD]
        ct[rows] = piece
        for k in range(HEADS):
            ctbig[rows, k * HEAD : (k + 1) * HEAD] = piece if k == h else jnp.zeros_like(piece)
    gram[...] = jnp.where(block, mm(at[...], bt[...], NT), 0.0).astype(BF)
    kk[...] = jnp.where(block, mm(ct[...], ct[...], NT), 0.0).astype(BF)
    wop[...] = mm(ctbig[...], wo[...]).astype(BF)
    causal = iota((STEPS, STEPS), 0) >= iota((STEPS, STEPS), 1)
    for b in range(LB):
        for h in range(HEADS):
            diff = gcol[b][:, h * PATCH : h * PATCH + 1] - growth[b * HEADS + h : b * HEADS + h + 1]
            decay[b * HEADS + h] = jnp.where(causal, jnp.exp(diff), 0.0)

    pltpu.make_async_copy(recv_mix, recv_mix, mix_r).wait()
    spread = (lax.rem(iota((HEAD, HEAD), 0), PATCH) == lax.rem(iota((HEAD, HEAD), 1), PATCH)).astype(BF)
    pick = (iota((STEPS, 64), 0) // 4 == iota((STEPS, 64), 1)).astype(BF)
    mine = lax.rem(iota((STEPS, HEAD), 0), 4) == iota((STEPS, HEAD), 1) // PATCH
    for b in range(LB):
        packed = ((recv_mix[0, b] + recv_mix[1, b]) + (recv_mix[2, b] + recv_mix[3, b])).astype(BF)
        lone = jnp.where(mine, mm(pick, packed), 0.0).astype(BF)
        rows = mm(lone, spread)
        m4[pl.ds(b * STEPS, STEPS)] = rows.astype(BF)
        faded = (rows * fade[b]).astype(BF)
        m_local[pl.ds(b * PATCH, PATCH)] = mm(rows.astype(BF), faded, TN)[:PATCH]
    ctx_rows(spare_m, m_local, recv_m, m_s, m_r, lambda other: 2 * other, 2 * ctx)

    def inside(b):
        rows = pl.ds(b * STEPS, STEPS)
        mb = m4[rows]
        mg = mm(mb, gram[...])
        mgs[rows] = (mg * rise[b]).astype(BF)
        mgb = mg.astype(BF)
        total = jnp.zeros((STEPS, HEAD), F32)
        for h in range(HEADS):
            score = mm(jnp.where(heads[h], mgb, jnp.zeros_like(mgb)), mb, NT)
            score = (score * decay[b * HEADS + h]).astype(BF)
            total = total + mm(score, jnp.where(heads[h], mb, jnp.zeros_like(mb)))
        u_ref[rows] = total

    inside(0)
    cot_load.wait()
    y0[...] = mm(cot[...], wop[...], NT)

    pltpu.make_async_copy(recv_g, recv_g, g_r).wait()
    pltpu.make_async_copy(recv_m, recv_m, m_r).wait()
    own_b = ctx // (NCTX // LB)
    state = jnp.zeros((2, HEAD), F32)
    for j in range(NCTX):
        stage_s[2 * j : 2 * j + 2] = state
        state = jnp.exp(recv_g[pl.ds(2 * j + own_b, 1)]) * state + recv_m[2 * j : 2 * j + 2]
    ctx_rows(spare_s, stage_s, recv_s, s_s, s_r, lambda other: 2 * other, 2 * ctx)
    inside(1)
    pltpu.make_async_copy(recv_s, recv_s, s_r).wait()

    memory = []
    for b in range(LB):
        part = recv_s[pl.ds(b * PATCH, PATCH)]
        memory.append(
            jnp.where(block, jnp.concatenate([part] * HEADS, axis=0), 0.0).astype(BF)
        )
        rows = pl.ds(b * STEPS, STEPS)
        u_ref[rows] = u_ref[rows] + mm(mgs[rows], memory[b])
    u = u_ref[...]
    ub = u.astype(BF)
    read = mm(ub, ctbig[...])
    sums = (iota((WIDTH, HEAD), 0) // HEAD == iota((WIDTH, HEAD), 1) // PATCH).astype(BF)
    square = mm((read * read).astype(BF), sums) * (1.0 / HEAD)
    inv = lax.rsqrt(square + EPS)
    n = u * inv
    nb = n.astype(BF)
    dots = mm((y0[...] * u).astype(BF), block.astype(BF)) * (1.0 / HEAD)
    def repeat(square_block):
        kept = jnp.where(block, square_block, 0.0)
        kept = kept + pltpu.roll(kept, 64, 1)
        return kept + pltpu.roll(kept, 32, 1)

    def scatter(source, target, send, recv, partners):
        for other, level in partners:
            pltpu.make_async_remote_copy(
                source.at[pl.ds(other * NMIX + level, 1)], target.at[pl.ds(me, 1)], send, recv,
                device_id=(other, level), device_id_type=MESH,
            ).start()

    zall[:, :WIDTH] = mm(nb, cot[...], TN)
    zall[:, WIDTH:] = repeat(mm((n * (inv * dots)).astype(BF), nb, TN))
    pltpu.make_async_copy(zall.at[pl.ds(me, 1)], recv_z.at[pl.ds(me, 1)], z_r).start()
    spare_copy(zall.at[pl.ds(me, 1)], spare_z, z_s)
    scatter(zall, recv_z, z_s, z_r, all_partners[:7])

    y = inv * (y0[...] - inv * (inv * dots) * mm(ub, kk[...]))
    y_ref[...] = y
    for b in range(LB):
        rows = pl.ds(b * STEPS, STEPS)
        mb = m4[rows]
        yb = y_ref[rows]
        yh = yb.astype(BF)
        total = mm((yb * rise[b]).astype(BF), memory[b])
        for h in range(HEADS):
            share = 7 + 15 * (b * HEADS + h)
            scatter(zall, recv_z, z_s, z_r, all_partners[share : share + 15])
            left = mm(jnp.where(heads[h], yh, jnp.zeros_like(yh)), mb, NT)
            left = (left * decay[b * HEADS + h]).astype(BF)
            total = total + mm(left, jnp.where(heads[h], mb, jnp.zeros_like(mb)))
        a_ref[rows] = total.astype(BF)
    xall[...] = repeat(mm(m4[...], a_ref[...], TN))
    scatter(xall, recv_x, x_s, x_r, all_partners)
    pltpu.make_async_copy(xall.at[pl.ds(me, 1)], recv_x.at[pl.ds(me, 1)], x_r).start()
    spare_copy(xall.at[pl.ds(me, 1)], spare_x, x_s)

    out[...] = mm(nb, wop[...]).astype(BF)

    w_head = wo[pl.ds(plane * HEAD, HEAD)]
    c_head = ct[pl.ds(plane * PATCH, PATCH)]
    chosen = (iota((16, HEAD), 1) == 16 * lax.rem(ctx, 8) + iota((16, HEAD), 0)).astype(BF)
    c_rows = mm(chosen, c_head, NT).astype(BF)
    column = (iota((16, WIDTH), 1) == ctx * 16 + iota((16, WIDTH), 0)).astype(BF)
    embed_rows = mm(column, jnp.concatenate([we[...]] * HEADS, axis=0), NT).astype(BF)
    tall = jnp.concatenate([jnp.where(heads[h], embed_rows, jnp.zeros_like(embed_rows)) for h in range(HEADS)], axis=0)
    qkv_rows = wq[pl.ds(ctx * 16, 16)]
    long = jnp.concatenate(
        [
            jnp.concatenate(
                [qkv_rows[:, j * WIDTH + h * HEAD : j * WIDTH + (h + 1) * HEAD] for j in range(3)], axis=1
            )
            for h in range(HEADS)
        ],
        axis=0,
    )

    pltpu.make_async_copy(recv_z, recv_z, z_r).wait()
    row = jnp.sum(recv_z[...], axis=0, keepdims=True)
    fine = row[:, :WIDTH]
    zrow[...] = fine
    local = lax.rem(me, NCTX)

    for partner in plane_partners:
        pltpu.make_async_remote_copy(
            zrow, recv_zh.at[pl.ds(local, 1)], zh_s, zh_r, device_id=partner, device_id_type=MESH
        ).start()
    spare_copy(zrow, spare_zh, zh_s)
    pltpu.make_async_copy(zrow, recv_zh.at[pl.ds(local, 1)], zh_r).start()

    high = fine.astype(BF)
    low = (fine - high.astype(F32)).astype(BF)
    yxrow[:, :HEAD] = mm(high, w_head, NT) + mm(low, w_head, NT) - mm(row[:, WIDTH : WIDTH + PATCH].astype(BF), c_head)
    pltpu.make_async_copy(recv_x, recv_x, x_r).wait()
    yxrow[:, HEAD:] = jnp.sum(recv_x[...], axis=0, keepdims=True)
    for partner in all_partners:
        pltpu.make_async_remote_copy(
            yxrow, recv_yx.at[pl.ds(me, 1)], yx_s, yx_r, device_id=partner, device_id_type=MESH
        ).start()
    spare_copy(yxrow, spare_yx, yx_s)
    pltpu.make_async_copy(yxrow, recv_yx.at[pl.ds(me, 1)], yx_r).start()
    pltpu.make_async_copy(recv_yx, recv_yx, yx_r).wait()
    x_block = jnp.where(block, recv_yx[:, HEAD:], 0.0).astype(BF)
    yq = mm(x_block, bt[...])
    yk = mm(x_block, at[...], TN)
    ys = jnp.concatenate([yq, yk, recv_yx[:, :HEAD]], axis=1).astype(BF)
    wide = mm(tall, ys)
    for h in range(HEADS):
        for j in range(3):
            gqkv[:, j * WIDTH + h * HEAD : j * WIDTH + (h + 1) * HEAD] = wide[
                16 * h : 16 * h + 16, j * HEAD : (j + 1) * HEAD
            ]
    tops = mm(long, ys, NT)
    folded = jnp.zeros((16, HEAD), F32)
    for h in range(HEADS):
        folded = folded + jnp.where(heads[h], tops[16 * h : 16 * h + 16], 0.0)
    folded = folded + pltpu.roll(folded, 64, 1)
    folded = folded + pltpu.roll(folded, 32, 1)
    gemb[...] = folded[:, :PATCH]
    pltpu.make_async_copy(recv_zh, recv_zh, zh_r).wait()
    gout[...] = mm(c_rows, recv_zh[...].astype(BF))

    sent_mix = stage_mix.at[pl.ds(0, LB * (NMIX - 1))]
    pltpu.make_async_copy(sent_mix, sent_mix, mix_s).wait()
    for ref, sem in (
        (recv_g, g_s), (recv_m, m_s), (recv_s, s_s), (recv_z, z_s), (recv_x, x_s), (recv_yx, yx_s), (recv_zh, zh_s)
    ):
        pltpu.make_async_copy(ref, ref, sem).wait()


def hand_on(*refs):
    copies = [pltpu.make_async_copy(refs[i], refs[4 + i], refs[8].at[i]) for i in range(4)]
    for copy in copies:
        copy.start()
    for copy in copies:
        copy.wait()


def shards(
    sources, source_ids, mix_weights, source_lengths, w_embed, w_qkv, w_out, forget, cotangent
):
    packed = sources.reshape(LOCAL_SOURCES, STEPS * PATCH // 128, 128).transpose(1, 0, 2)
    vm = pltpu.VMEM
    sm = pltpu.SMEM
    dma = pltpu.SemaphoreType.DMA
    results = pl.pallas_call(
        kernel,
        out_shape=tuple(vm(shape, kind) for shape, kind in RESULTS),
        in_specs=[pl.BlockSpec(memory_space=pl.ANY)] * 9,
        out_specs=(pl.BlockSpec(memory_space=pltpu.VMEM),) * 4,
        scratch_shapes=[
            vm((LOCAL_SOURCES, 64, 128), F32),
            sm((TERMS, LB * NMIX), jnp.int32),
            sm((TERMS, LB * NMIX), F32),
            sm((TERMS, LB * NMIX), jnp.int32),
            vm((PATCH, WIDTH), BF),
            vm((WIDTH, 3 * WIDTH), BF),
            vm((WIDTH, WIDTH), BF),
            vm((LB * HEADS, STEPS), F32),
            vm((ROWS, WIDTH), BF),
            vm((LB * NMIX, 64, 128), F32),
            vm((NMIX, LB, 64, 128), F32),
            vm((LB, HEAD), F32),
            vm((2 * NCTX, HEAD), F32),
            vm((2 * NCTX, HEAD), F32),
            vm((2 * NCTX, HEAD), F32),
            vm((2 * NCTX, HEAD), F32),
            vm((2 * NCTX, HEAD), F32),
            vm((LB, STEPS, HEAD), F32),
            vm((LB, STEPS, HEAD), F32),
            vm((LB * HEADS, STEPS, STEPS), F32),
            vm((ROWS, HEAD), BF),
            vm((ROWS, HEAD), BF),
            vm((ROWS, HEAD), F32),
            vm((ROWS, HEAD), BF),
            vm((ROWS, HEAD), F32),
            vm((LB, STEPS, HEAD), F32),
            vm((HEAD, HEAD), BF),
            vm((HEAD, HEAD), BF),
            vm((HEAD, HEAD), BF),
            vm((HEAD, WIDTH), BF),
            vm((HEAD, HEAD), BF),
            vm((HEAD, HEAD), BF),
            vm((HEAD, WIDTH), BF),
            vm((ROWS, HEAD), F32),
            vm((NDEV, VX), F32),
            vm((NDEV, VX), F32),
            vm((NDEV, HEAD), F32),
            vm((NDEV, HEAD), F32),
            vm((1, WIDTH), F32),
            vm((NCTX, WIDTH), F32),
            vm((1, 2 * HEAD), F32),
            vm((NDEV, 2 * HEAD), F32),
            vm((2, HEAD), F32),
            vm((2, HEAD), F32),
            vm((2, HEAD), F32),
            vm((1, VX), F32),
            vm((1, HEAD), F32),
            vm((1, 2 * HEAD), F32),
            vm((1, WIDTH), F32),
            dma((13,)),
        ]
        + [dma(())] * 16,
        compiler_params=pltpu.CompilerParams(collective_id=0, has_side_effects=True, vmem_limit_bytes=60 << 20),
        name="whole_step",
    )(
        packed, source_ids.T, mix_weights.T, source_lengths.T, w_embed.T, w_qkv, w_out, forget,
        cotangent.reshape(ROWS, WIDTH),
    )
    output, grad_qkv, grad_out, grad_embed = pl.pallas_call(
        hand_on,
        out_shape=tuple(jax.ShapeDtypeStruct(shape, kind) for shape, kind in RESULTS),
        in_specs=[pl.BlockSpec(memory_space=pltpu.VMEM)] * 4,
        out_specs=(pl.BlockSpec(memory_space=pl.ANY),) * 4,
        scratch_shapes=[dma((4,))],
        name="hand_on",
    )(*[pltpu.with_memory_space_constraint(result, pltpu.VMEM) for result in results])
    return (output.reshape(LB, STEPS, WIDTH), grad_qkv, grad_out, grad_embed)


def solution(mesh):
    placed = (
        P("mix", "ctx"),
        P(),
        P(),
        P(),
        P(),
        P(),
        P(),
        P("mix", None, "ctx"),
        P("mix", "ctx", None),
    )
    return jax.shard_map(
        shards,
        mesh=mesh,
        in_specs=placed,
        out_specs=(P("mix", "ctx", None), P("ctx", None), P("ctx", None), P("ctx", None)),
        check_vma=False,
    )
```

time: 48.4 us -> 42.5 us (0.88)
  Pallas kernels: 47.7 us -> 41.8 us
    pallas_call x2, Pallas kernels: 47.7 us -> 41.8 us  [the longest x1 40.9 us: shards(): pl.pallas_call(kernel, out_shape=tuple((vm(shape, kind) for shape, kind i...]
where the time goes in v3:
time: 42.5 us; the launch traced here: 42.4 us
  Pallas kernels  41.8 us (98%)
  between operations  0.64 us (2%)
    pallas_call x1, Pallas kernels, shards(): pl.pallas_call(kernel, out_shape=tuple((vm(shape, kind) for shape, kind i...  40.9 us
    pallas_call x1, Pallas kernels, shards(): pl.pallas_call(hand_on, out_shape=tuple((jax.ShapeDtypeStruct(shape, kind...  0.86 us

profile of v3, /device:TPU:1, one launch (start us, length us, event | category | flops | bytes accessed | tf_op | source)
XLA Modules:
  0.0 42.4 jit_solution(12411281085918464567)
XLA Ops:
  0.6 40.9 %whole_step.1 = (bf16[512,512]{1,0:T(8,128)(2,1)S(1)}, f32[16,1536]{1,0:T(8,128)S(1)}, f32[16,512]{1,0:T(8,128)S(1)}, f32[16,32]{1,0:T(8,128)S(1)}) custom-call(f32[64,4,128]{2,1,0:T(4,128)} %bitcast.10, s32[3,8]{1,0:T(4,128)} %bitcast.12, f32[3,8]{1,0:T(4,128)} %bitcast.13, s32[3,8]{1,0:T(4,128)} %bitcast.14, bf16[32,512]{1,0:T(8,128)(2,1)} %bitcast.11, ...), custom_call_target="tpu_custom_call" | custom-call | tf_op jit(solution)/shard_map/whole_step/pallas_call | solution.py:365
  41.6 0.9 %hand_on.1 = (bf16[512,512]{1,0:T(8,128)(2,1)}, f32[16,1536]{1,0:T(8,128)}, f32[16,512]{1,0:T(8,128)}, f32[16,32]{1,0:T(8,128)}) custom-call(bf16[512,512]{1,0:T(8,128)(2,1)S(1)} %get-tuple-element.12.refs_0_, f32[16,1536]{1,0:T(8,128)S(1)} %get-tuple-element.13.refs_1_, f32[16,512]{1,0:T(8,128)S(1)} %get-tuple-element.14.refs_2_, ...), custom_call_target="tpu_custom_call" | custom-call | tf_op jit(solution)/shard_map/hand_on/pallas_call | solution.py:429

commit v4 on v3

--- a/solution.py
+++ b/solution.py
@@ -12,6 +12,8 @@
 NCTX = 32
 NMIX = 4
 NDEV = 128
+ROW = 8
+PLANES = 4
 LB = 2
 HEADS = 4
 PATCH = 32
@@ -61,11 +63,11 @@
     src_hbm, ids_hbm, wts_hbm, lens_hbm, we_hbm, wq_hbm, wo_hbm, forget_hbm, cot_hbm,
     out, gqkv, gout, gemb,
     src, ids, wts, lens, we, wq, wo, forget, cot,
-    stage_mix, recv_mix, glast, recv_g, m_local, recv_m, stage_s, recv_s,
-    rise, fade, decay, m4, mgs, u_ref, a_ref, y_ref, gcol, at, bt, ct, ctbig, gram, kk, wop, y0,
-    zall, recv_z, xall, recv_x, zrow, recv_zh, yxrow, recv_yx,
-    spare_g, spare_m, spare_s, spare_z, spare_x, spare_yx, spare_zh,
-    in_sem, mix_s, mix_r, g_s, g_r, m_s, m_r, s_s, s_r, z_s, z_r, x_s, x_r, zh_s, zh_r, yx_s, yx_r,
+    stage_mix, recv_mix, glast, recv_g, row_gate, recv_r, m_local, recv_m, stage_s, stage_t, recv_s,
+    rise, fade, decay, m4, mgs, mgp, u_ref, a_ref, y_ref, gcol, at, bt, ct, ctbig, gram, kk, wop, y0,
+    zall, recv_z, zrow, recv_zh, yxrow, recv_yx,
+    spare_g, spare_r, spare_m, spare_s, spare_z, spare_yx, spare_zh,
+    in_sem, mix_s, mix_r, g_s, g_r, r_s, r_r, m_s, m_r, s_s, s_r, z_s, z_r, zh_s, zh_r, yx_s, yx_r,
 ):
     ctx = lax.axis_index("ctx")
     mix = lax.axis_index("mix")
@@ -87,15 +89,19 @@
     xs = [lax.rem(ctx // 2 + d, 4) * 2 for d in range(4)]
     cs = [lax.rem(ctx + d, 2) for d in range(2)]
     zs = [lax.rem(mix + d, NMIX) for d in range(NMIX)]
-    ctx_partners = [ys[y] + xs[x] + cs[c] for y, x, c in CTX_STEPS]
     all_partners = [(ys[y] + xs[x] + cs[c], zs[z]) for y, x, c, z in ALL_STEPS]
     plane_partners = [(ys[y] + xs[x] + cs[c], zs[z]) for y, x, c, z in ALL_STEPS if y == 0]
 
+    place_x = lax.rem(ctx, 8)
+    row_partners = [(xs[x] + cs[c]) for y, x, c in CTX_STEPS if y == 0]
+
     barrier = pltpu.get_barrier_semaphore()
-    for other in ctx_partners:
-        pl.semaphore_signal(barrier, inc=1, device_id=(other, mix), device_id_type=MESH)
-    for other in zs[1:]:
-        pl.semaphore_signal(barrier, inc=1, device_id=(ctx, other), device_id_type=MESH)
+    for level in zs[1:]:
+        pl.semaphore_signal(barrier, inc=1, device_id=(ctx, level), device_id_type=MESH)
+    for other in row_partners:
+        pl.semaphore_signal(barrier, inc=1, device_id=(ys[0] + other, mix), device_id_type=MESH)
+    for base in ys[1:]:
+        pl.semaphore_signal(barrier, inc=1, device_id=(base + place_x, mix), device_id_type=MESH)
 
     for load in part_loads:
         load.wait()
@@ -109,7 +115,7 @@
             part = part + jnp.where(place < lens[j, b], weight, 0.0) * src[held]
         stage_mix[b] = part
 
-    pl.semaphore_wait(barrier, NCTX - 1 + NMIX - 1)
+    pl.semaphore_wait(barrier, NMIX - 1 + ROW - 1 + PLANES - 1)
 
     own_mix = pltpu.make_async_copy(stage_mix.at[pl.ds(LB * mix, LB)], recv_mix.at[mix], mix_r)
     own_mix.start()
@@ -122,15 +128,9 @@
     def spare_copy(part, spare, send):
         pltpu.make_async_copy(part, spare, send).start()
 
-    def ctx_rows(spare, src_ref, dst_ref, send, recv, src_row, dst_row):
-        for other in ctx_partners:
-            pltpu.make_async_remote_copy(
-                src_ref.at[pl.ds(src_row(other), 2)], dst_ref.at[pl.ds(dst_row, 2)], send, recv,
-                device_id=(other, mix), device_id_type=MESH,
-            ).start()
-        spare_copy(src_ref.at[pl.ds(src_row(ctx), 2)], spare, send)
-        pltpu.make_async_copy(
-            src_ref.at[pl.ds(src_row(ctx), 2)], dst_ref.at[pl.ds(dst_row, 2)], recv
+    def push(source, target, send, recv, other, level):
+        pltpu.make_async_remote_copy(
+            source, target, send, recv, device_id=(other, level), device_id_type=MESH
         ).start()
 
     for load in gate_loads:
@@ -153,7 +153,11 @@
         rise[b] = jnp.exp(col)
         fade[b] = jnp.exp(last - col)
 
-    ctx_rows(spare_g, glast, recv_g, g_s, g_r, lambda other: 0, 2 * ctx)
+    own_g = recv_g.at[pl.ds(LB * place_x, LB)]
+    for other in row_partners:
+        push(glast, own_g, g_s, g_r, ys[0] + other, mix)
+    pltpu.make_async_copy(glast, own_g, g_r).start()
+    spare_copy(glast, spare_g, g_s)
 
     for load in weight_loads:
         load.wait()
@@ -178,6 +182,20 @@
             diff = gcol[b][:, h * PATCH : h * PATCH + 1] - growth[b * HEADS + h : b * HEADS + h + 1]
             decay[b * HEADS + h] = jnp.where(causal, jnp.exp(diff), 0.0)
 
+    pltpu.make_async_copy(recv_g, recv_g, g_r).wait()
+    gates = [recv_g[LB * q : LB * q + LB] for q in range(ROW)]
+    inner = jnp.zeros((LB, HEAD), F32)
+    whole = jnp.zeros((LB, HEAD), F32)
+    for q in range(ROW):
+        inner = inner + jnp.where(q < place_x, gates[q], 0.0)
+        whole = whole + gates[q]
+    row_gate[...] = whole
+    own_r = recv_r.at[pl.ds(LB * plane, LB)]
+    for base in ys[1:]:
+        push(row_gate, own_r, r_s, r_r, base + place_x, mix)
+    pltpu.make_async_copy(row_gate, own_r, r_r).start()
+    spare_copy(row_gate, spare_r, r_s)
+
     pltpu.make_async_copy(recv_mix, recv_mix, mix_r).wait()
     spread = (lax.rem(iota((HEAD, HEAD), 0), PATCH) == lax.rem(iota((HEAD, HEAD), 1), PATCH)).astype(BF)
     pick = (iota((STEPS, 64), 0) // 4 == iota((STEPS, 64), 1)).astype(BF)
@@ -189,39 +207,67 @@
         m4[pl.ds(b * STEPS, STEPS)] = rows.astype(BF)
         faded = (rows * fade[b]).astype(BF)
         m_local[pl.ds(b * PATCH, PATCH)] = mm(rows.astype(BF), faded, TN)[:PATCH]
-    ctx_rows(spare_m, m_local, recv_m, m_s, m_r, lambda other: 2 * other, 2 * ctx)
-
-    def inside(b):
+    own_m = recv_m.at[place_x]
+    for other in row_partners:
+        push(m_local.at[pl.ds(8 * other, 8)], own_m, m_s, m_r, ys[0] + other, mix)
+    mine_m = m_local.at[pl.ds(8 * place_x, 8)]
+    pltpu.make_async_copy(mine_m, own_m, m_r).start()
+    spare_copy(mine_m, spare_m, m_s)
+
+    def scores(b):
         rows = pl.ds(b * STEPS, STEPS)
-        mb = m4[rows]
-        mg = mm(mb, gram[...])
+        mg = mm(m4[rows], gram[...])
+        mgp[rows] = mg.astype(BF)
         mgs[rows] = (mg * rise[b]).astype(BF)
-        mgb = mg.astype(BF)
-        total = jnp.zeros((STEPS, HEAD), F32)
-        for h in range(HEADS):
+
+    def inside(b, some, total):
+        rows = pl.ds(b * STEPS, STEPS)
+        mb, mgb = m4[rows], mgp[rows]
+        for h in some:
             score = mm(jnp.where(heads[h], mgb, jnp.zeros_like(mgb)), mb, NT)
             score = (score * decay[b * HEADS + h]).astype(BF)
-            total = total + mm(score, jnp.where(heads[h], mb, jnp.zeros_like(mb)))
+            part = mm(score, jnp.where(heads[h], mb, jnp.zeros_like(mb)))
+            total = part if total is None else total + part
         u_ref[rows] = total
 
-    inside(0)
+    scores(0)
+    inside(0, (0, 1), None)
+
+    pltpu.make_async_copy(recv_m, recv_m, m_r).wait()
+    own_b = place_x // (ROW // LB)
+    state = jnp.zeros((8, HEAD), F32)
+    for q in range(ROW):
+        stage_s[q] = state
+        state = jnp.exp(recv_g[pl.ds(LB * q + own_b, 1)]) * state + recv_m[q]
+    stage_t[...] = state
+    own_s = recv_s.at[plane, place_x]
+    for y, x, c in CTX_STEPS:
+        other = xs[x] + cs[c]
+        push(stage_s.at[other] if y == 0 else stage_t, own_s, s_s, s_r, ys[y] + other, mix)
+    pltpu.make_async_copy(stage_s.at[place_x], own_s, s_r).start()
+    spare_copy(stage_t, spare_s, s_s)
+
+    inside(0, (2, 3), u_ref[pl.ds(0, STEPS)])
+    scores(1)
+    inside(1, range(HEADS), None)
     cot_load.wait()
     y0[...] = mm(cot[...], wop[...], NT)
-
-    pltpu.make_async_copy(recv_g, recv_g, g_r).wait()
-    pltpu.make_async_copy(recv_m, recv_m, m_r).wait()
-    own_b = ctx // (NCTX // LB)
-    state = jnp.zeros((2, HEAD), F32)
-    for j in range(NCTX):
-        stage_s[2 * j : 2 * j + 2] = state
-        state = jnp.exp(recv_g[pl.ds(2 * j + own_b, 1)]) * state + recv_m[2 * j : 2 * j + 2]
-    ctx_rows(spare_s, stage_s, recv_s, s_s, s_r, lambda other: 2 * other, 2 * ctx)
-    inside(1)
+    pltpu.make_async_copy(recv_r, recv_r, r_r).wait()
+    factors = []
+    reach = inner
+    for back in range(PLANES):
+        factors.append(reach)
+        if back < PLANES - 1:
+            reach = reach + recv_r[pl.ds(LB * jnp.maximum(plane - 1 - back, 0), LB)]
     pltpu.make_async_copy(recv_s, recv_s, s_r).wait()
 
     memory = []
     for b in range(LB):
-        part = recv_s[pl.ds(b * PATCH, PATCH)]
+        part = recv_s[plane, b * 4 : b * 4 + 4].reshape(PATCH, HEAD)
+        for back in range(1, PLANES):
+            earlier = recv_s[jnp.maximum(plane - back, 0), b * 4 : b * 4 + 4].reshape(PATCH, HEAD)
+            weight = jnp.where(plane >= back, jnp.exp(factors[back - 1][b : b + 1]), 0.0)
+            part = part + weight * earlier
         memory.append(
             jnp.where(block, jnp.concatenate([part] * HEADS, axis=0), 0.0).astype(BF)
         )
@@ -236,25 +282,8 @@
     n = u * inv
     nb = n.astype(BF)
     dots = mm((y0[...] * u).astype(BF), block.astype(BF)) * (1.0 / HEAD)
-    def repeat(square_block):
-        kept = jnp.where(block, square_block, 0.0)
-        kept = kept + pltpu.roll(kept, 64, 1)
-        return kept + pltpu.roll(kept, 32, 1)
-
-    def scatter(source, target, send, recv, partners):
-        for other, level in partners:
-            pltpu.make_async_remote_copy(
-                source.at[pl.ds(other * NMIX + level, 1)], target.at[pl.ds(me, 1)], send, recv,
-                device_id=(other, level), device_id_type=MESH,
-            ).start()
-
-    zall[:, :WIDTH] = mm(nb, cot[...], TN)
-    zall[:, WIDTH:] = repeat(mm((n * (inv * dots)).astype(BF), nb, TN))
-    pltpu.make_async_copy(zall.at[pl.ds(me, 1)], recv_z.at[pl.ds(me, 1)], z_r).start()
-    spare_copy(zall.at[pl.ds(me, 1)], spare_z, z_s)
-    scatter(zall, recv_z, z_s, z_r, all_partners[:7])
-
-    y = inv * (y0[...] - inv * (inv * dots) * mm(ub, kk[...]))
+    drift = inv * (inv * dots)
+    y = inv * (y0[...] - drift * mm(ub, kk[...]))
     y_ref[...] = y
     for b in range(LB):
         rows = pl.ds(b * STEPS, STEPS)
@@ -263,16 +292,28 @@
         yh = yb.astype(BF)
         total = mm((yb * rise[b]).astype(BF), memory[b])
         for h in range(HEADS):
-            share = 7 + 15 * (b * HEADS + h)
-            scatter(zall, recv_z, z_s, z_r, all_partners[share : share + 15])
             left = mm(jnp.where(heads[h], yh, jnp.zeros_like(yh)), mb, NT)
             left = (left * decay[b * HEADS + h]).astype(BF)
             total = total + mm(left, jnp.where(heads[h], mb, jnp.zeros_like(mb)))
         a_ref[rows] = total.astype(BF)
-    xall[...] = repeat(mm(m4[...], a_ref[...], TN))
-    scatter(xall, recv_x, x_s, x_r, all_partners)
-    pltpu.make_async_copy(xall.at[pl.ds(me, 1)], recv_x.at[pl.ds(me, 1)], x_r).start()
-    spare_copy(xall.at[pl.ds(me, 1)], spare_x, x_s)
+
+    def repeat(square_block):
+        kept = jnp.where(block, square_block, 0.0)
+        kept = kept + pltpu.roll(kept, 64, 1)
+        return kept + pltpu.roll(kept, 32, 1)
+
+    zall[:, :WIDTH] = mm(nb, cot[...], TN)
+    v_rows = repeat(mm((n * (inv * dots)).astype(BF), nb, TN))
+    x_rows = repeat(mm(m4[...], a_ref[...], TN))
+    zall[:, WIDTH:] = jnp.where(lane < 64, v_rows, x_rows)
+
+    for other, level in all_partners:
+        pltpu.make_async_remote_copy(
+            zall.at[pl.ds(other * NMIX + level, 1)], recv_z.at[pl.ds(me, 1)], z_s, z_r,
+            device_id=(other, level), device_id_type=MESH,
+        ).start()
+    spare_copy(zall.at[pl.ds(me, 1)], spare_z, z_s)
+    pltpu.make_async_copy(zall.at[pl.ds(me, 1)], recv_z.at[pl.ds(me, 1)], z_r).start()
 
     out[...] = mm(nb, wop[...]).astype(BF)
 
@@ -296,8 +337,22 @@
 
     pltpu.make_async_copy(recv_z, recv_z, z_r).wait()
     row = jnp.sum(recv_z[...], axis=0, keepdims=True)
+    zrow[...] = row[:, :WIDTH]
+    mixed = row[:, WIDTH:]
     fine = row[:, :WIDTH]
-    zrow[...] = fine
+    high = fine.astype(BF)
+    low = (fine - high.astype(F32)).astype(BF)
+    yv = mm(high, w_head, NT) + mm(low, w_head, NT) - mm(mixed[:, :PATCH].astype(BF), c_head)
+    xs = jnp.where(lane < 64, 0.0, mixed)
+    yxrow[:, :HEAD] = yv
+    yxrow[:, HEAD:] = xs + pltpu.roll(xs, 64, 1)
+
+    for partner in all_partners:
+        pltpu.make_async_remote_copy(
+            yxrow, recv_yx.at[pl.ds(me, 1)], yx_s, yx_r, device_id=partner, device_id_type=MESH
+        ).start()
+    spare_copy(yxrow, spare_yx, yx_s)
+    pltpu.make_async_copy(yxrow, recv_yx.at[pl.ds(me, 1)], yx_r).start()
     local = lax.rem(me, NCTX)
 
     for partner in plane_partners:
@@ -307,17 +362,6 @@
     spare_copy(zrow, spare_zh, zh_s)
     pltpu.make_async_copy(zrow, recv_zh.at[pl.ds(local, 1)], zh_r).start()
 
-    high = fine.astype(BF)
-    low = (fine - high.astype(F32)).astype(BF)
-    yxrow[:, :HEAD] = mm(high, w_head, NT) + mm(low, w_head, NT) - mm(row[:, WIDTH : WIDTH + PATCH].astype(BF), c_head)
-    pltpu.make_async_copy(recv_x, recv_x, x_r).wait()
-    yxrow[:, HEAD:] = jnp.sum(recv_x[...], axis=0, keepdims=True)
-    for partner in all_partners:
-        pltpu.make_async_remote_copy(
-            yxrow, recv_yx.at[pl.ds(me, 1)], yx_s, yx_r, device_id=partner, device_id_type=MESH
-        ).start()
-    spare_copy(yxrow, spare_yx, yx_s)
-    pltpu.make_async_copy(yxrow, recv_yx.at[pl.ds(me, 1)], yx_r).start()
     pltpu.make_async_copy(recv_yx, recv_yx, yx_r).wait()
     x_block = jnp.where(block, recv_yx[:, HEAD:], 0.0).astype(BF)
     yq = mm(x_block, bt[...])
@@ -342,7 +386,7 @@
     sent_mix = stage_mix.at[pl.ds(0, LB * (NMIX - 1))]
     pltpu.make_async_copy(sent_mix, sent_mix, mix_s).wait()
     for ref, sem in (
-        (recv_g, g_s), (recv_m, m_s), (recv_s, s_s), (recv_z, z_s), (recv_x, x_s), (recv_yx, yx_s), (recv_zh, zh_s)
+        (recv_g, g_s), (recv_r, r_s), (recv_m, m_s), (recv_s, s_s), (recv_z, z_s), (recv_yx, yx_s), (recv_zh, zh_s)
     ):
         pltpu.make_async_copy(ref, ref, sem).wait()
 
@@ -380,14 +424,18 @@
             vm((LB * NMIX, 64, 128), F32),
             vm((NMIX, LB, 64, 128), F32),
             vm((LB, HEAD), F32),
-            vm((2 * NCTX, HEAD), F32),
-            vm((2 * NCTX, HEAD), F32),
-            vm((2 * NCTX, HEAD), F32),
-            vm((2 * NCTX, HEAD), F32),
-            vm((2 * NCTX, HEAD), F32),
+            vm((LB * ROW, HEAD), F32),
+            vm((LB, HEAD), F32),
+            vm((LB * PLANES, HEAD), F32),
+            vm((LB * PATCH, HEAD), F32),
+            vm((ROW, 8, HEAD), F32),
+            vm((ROW, 8, HEAD), F32),
+            vm((8, HEAD), F32),
+            vm((PLANES, ROW, 8, HEAD), F32),
             vm((LB, STEPS, HEAD), F32),
             vm((LB, STEPS, HEAD), F32),
             vm((LB * HEADS, STEPS, STEPS), F32),
+            vm((ROWS, HEAD), BF),
             vm((ROWS, HEAD), BF),
             vm((ROWS, HEAD), BF),
             vm((ROWS, HEAD), F32),
@@ -404,17 +452,15 @@
             vm((ROWS, HEAD), F32),
             vm((NDEV, VX), F32),
             vm((NDEV, VX), F32),
-            vm((NDEV, HEAD), F32),
-            vm((NDEV, HEAD), F32),
             vm((1, WIDTH), F32),
             vm((NCTX, WIDTH), F32),
             vm((1, 2 * HEAD), F32),
             vm((NDEV, 2 * HEAD), F32),
-            vm((2, HEAD), F32),
-            vm((2, HEAD), F32),
-            vm((2, HEAD), F32),
+            vm((LB, HEAD), F32),
+            vm((LB, HEAD), F32),
+            vm((8, HEAD), F32),
+            vm((8, HEAD), F32),
             vm((1, VX), F32),
-            vm((1, HEAD), F32),
             vm((1, 2 * HEAD), F32),
             vm((1, WIDTH), F32),
             dma((13,)),

time: 42.5 us -> 39.9 us (0.939)
  Pallas kernels: 41.8 us -> 39.1 us
    pallas_call x1, Pallas kernels: 40.9 us -> 38.3 us  [shards(): pl.pallas_call(kernel, out_shape=tuple((vm(shape, kind) for shape, kind i...]
where the time goes in v4:
time: 39.9 us; the launch traced here: 39.8 us
  Pallas kernels  39.1 us (98%)
  between operations  0.64 us (2%)
    pallas_call x1, Pallas kernels, shards(): pl.pallas_call(kernel, out_shape=tuple((vm(shape, kind) for shape, kind i...  38.3 us
    pallas_call x1, Pallas kernels, shards(): pl.pallas_call(hand_on, out_shape=tuple((jax.ShapeDtypeStruct(shape, kind...  0.86 us

profile of v4, /device:TPU:1, one launch (start us, length us, event | category | flops | bytes accessed | tf_op | source)
XLA Modules:
  0.0 39.8 jit_solution(332621616306748219)
XLA Ops:
  0.6 38.3 %whole_step.1 = (bf16[512,512]{1,0:T(8,128)(2,1)S(1)}, f32[16,1536]{1,0:T(8,128)S(1)}, f32[16,512]{1,0:T(8,128)S(1)}, f32[16,32]{1,0:T(8,128)S(1)}) custom-call(f32[64,4,128]{2,1,0:T(4,128)} %bitcast.10, s32[3,8]{1,0:T(4,128)} %bitcast.12, f32[3,8]{1,0:T(4,128)} %bitcast.13, s32[3,8]{1,0:T(4,128)} %bitcast.14, bf16[32,512]{1,0:T(8,128)(2,1)} %bitcast.11, ...), custom_call_target="tpu_custom_call" | custom-call | tf_op jit(solution)/shard_map/whole_step/pallas_call | solution.py:409
  38.9 0.9 %hand_on.1 = (bf16[512,512]{1,0:T(8,128)(2,1)}, f32[16,1536]{1,0:T(8,128)}, f32[16,512]{1,0:T(8,128)}, f32[16,32]{1,0:T(8,128)}) custom-call(bf16[512,512]{1,0:T(8,128)(2,1)S(1)} %get-tuple-element.12.refs_0_, f32[16,1536]{1,0:T(8,128)S(1)} %get-tuple-element.13.refs_1_, f32[16,512]{1,0:T(8,128)S(1)} %get-tuple-element.14.refs_2_, ...), custom_call_target="tpu_custom_call" | custom-call | tf_op jit(solution)/shard_map/hand_on/pallas_call | solution.py:475

commit v5 on v4

--- a/solution.py
+++ b/solution.py
@@ -117,13 +117,14 @@
 
     pl.semaphore_wait(barrier, NMIX - 1 + ROW - 1 + PLANES - 1)
 
-    own_mix = pltpu.make_async_copy(stage_mix.at[pl.ds(LB * mix, LB)], recv_mix.at[mix], mix_r)
-    own_mix.start()
-    for other in (zs[2], zs[1], zs[3]):
-        pltpu.make_async_remote_copy(
-            stage_mix.at[pl.ds(LB * other, LB)], recv_mix.at[mix], mix_s, mix_r,
-            device_id=(ctx, other), device_id_type=MESH,
-        ).start()
+    for b in range(LB):
+        landing = recv_mix.at[b, mix]
+        for level in (zs[2], zs[1], zs[3]):
+            pltpu.make_async_remote_copy(
+                stage_mix.at[LB * level + b], landing, mix_s, mix_r.at[b],
+                device_id=(ctx, level), device_id_type=MESH,
+            ).start()
+        pltpu.make_async_copy(stage_mix.at[LB * mix + b], landing, mix_r.at[b]).start()
 
     def spare_copy(part, spare, send):
         pltpu.make_async_copy(part, spare, send).start()
@@ -174,7 +175,9 @@
         for k in range(HEADS):
             ctbig[rows, k * HEAD : (k + 1) * HEAD] = piece if k == h else jnp.zeros_like(piece)
     gram[...] = jnp.where(block, mm(at[...], bt[...], NT), 0.0).astype(BF)
-    kk[...] = jnp.where(block, mm(ct[...], ct[...], NT), 0.0).astype(BF)
+    square = jnp.where(block, mm(ct[...], ct[...], NT), 0.0)
+    kk[0] = square.astype(BF)
+    kk[1] = (square - kk[0].astype(F32)).astype(BF)
     wop[...] = mm(ctbig[...], wo[...]).astype(BF)
     causal = iota((STEPS, STEPS), 0) >= iota((STEPS, STEPS), 1)
     for b in range(LB):
@@ -196,12 +199,12 @@
     pltpu.make_async_copy(row_gate, own_r, r_r).start()
     spare_copy(row_gate, spare_r, r_s)
 
-    pltpu.make_async_copy(recv_mix, recv_mix, mix_r).wait()
     spread = (lax.rem(iota((HEAD, HEAD), 0), PATCH) == lax.rem(iota((HEAD, HEAD), 1), PATCH)).astype(BF)
     pick = (iota((STEPS, 64), 0) // 4 == iota((STEPS, 64), 1)).astype(BF)
     mine = lax.rem(iota((STEPS, HEAD), 0), 4) == iota((STEPS, HEAD), 1) // PATCH
     for b in range(LB):
-        packed = ((recv_mix[0, b] + recv_mix[1, b]) + (recv_mix[2, b] + recv_mix[3, b])).astype(BF)
+        pltpu.make_async_copy(recv_mix.at[b], recv_mix.at[b], mix_r.at[b]).wait()
+        packed = ((recv_mix[b, 0] + recv_mix[b, 1]) + (recv_mix[b, 2] + recv_mix[b, 3])).astype(BF)
         lone = jnp.where(mine, mm(pick, packed), 0.0).astype(BF)
         rows = mm(lone, spread)
         m4[pl.ds(b * STEPS, STEPS)] = rows.astype(BF)
@@ -275,15 +278,18 @@
         u_ref[rows] = u_ref[rows] + mm(mgs[rows], memory[b])
     u = u_ref[...]
     ub = u.astype(BF)
-    read = mm(ub, ctbig[...])
-    sums = (iota((WIDTH, HEAD), 0) // HEAD == iota((WIDTH, HEAD), 1) // PATCH).astype(BF)
-    square = mm((read * read).astype(BF), sums) * (1.0 / HEAD)
-    inv = lax.rsqrt(square + EPS)
+    ku = mm(ub, kk[0]) + mm(ub, kk[1])
+    ones = block.astype(BF)
+    square = ub.astype(F32) * ku
+    high = square.astype(BF)
+    low = (square - high.astype(F32)).astype(BF)
+    square = (mm(high, ones) + mm(low, ones)) * (1.0 / HEAD)
+    inv = lax.rsqrt(jnp.maximum(square, 0.0) + EPS)
     n = u * inv
     nb = n.astype(BF)
-    dots = mm((y0[...] * u).astype(BF), block.astype(BF)) * (1.0 / HEAD)
+    dots = mm((y0[...] * u).astype(BF), ones) * (1.0 / HEAD)
     drift = inv * (inv * dots)
-    y = inv * (y0[...] - drift * mm(ub, kk[...]))
+    y = inv * (y0[...] - drift * ku)
     y_ref[...] = y
     for b in range(LB):
         rows = pl.ds(b * STEPS, STEPS)
@@ -362,6 +368,8 @@
     spare_copy(zrow, spare_zh, zh_s)
     pltpu.make_async_copy(zrow, recv_zh.at[pl.ds(local, 1)], zh_r).start()
 
+    pltpu.make_async_copy(recv_zh, recv_zh, zh_r).wait()
+    gout[...] = mm(c_rows, recv_zh[...].astype(BF))
     pltpu.make_async_copy(recv_yx, recv_yx, yx_r).wait()
     x_block = jnp.where(block, recv_yx[:, HEAD:], 0.0).astype(BF)
     yq = mm(x_block, bt[...])
@@ -380,8 +388,6 @@
     folded = folded + pltpu.roll(folded, 64, 1)
     folded = folded + pltpu.roll(folded, 32, 1)
     gemb[...] = folded[:, :PATCH]
-    pltpu.make_async_copy(recv_zh, recv_zh, zh_r).wait()
-    gout[...] = mm(c_rows, recv_zh[...].astype(BF))
 
     sent_mix = stage_mix.at[pl.ds(0, LB * (NMIX - 1))]
     pltpu.make_async_copy(sent_mix, sent_mix, mix_s).wait()
@@ -392,7 +398,11 @@
 
 
 def hand_on(*refs):
-    copies = [pltpu.make_async_copy(refs[i], refs[4 + i], refs[8].at[i]) for i in range(4)]
+    moves = [(refs[i], refs[4 + i]) for i in range(1, 4)]
+    for i in range(4):
+        rows = pl.ds(i * ROWS // 4, ROWS // 4)
+        moves.append((refs[0].at[rows], refs[4].at[rows]))
+    copies = [pltpu.make_async_copy(a, b, refs[8].at[i]) for i, (a, b) in enumerate(moves)]
     for copy in copies:
         copy.start()
     for copy in copies:
@@ -422,7 +432,7 @@
             vm((LB * HEADS, STEPS), F32),
             vm((ROWS, WIDTH), BF),
             vm((LB * NMIX, 64, 128), F32),
-            vm((NMIX, LB, 64, 128), F32),
+            vm((LB, NMIX, 64, 128), F32),
             vm((LB, HEAD), F32),
             vm((LB * ROW, HEAD), F32),
             vm((LB, HEAD), F32),
@@ -447,7 +457,7 @@
             vm((HEAD, HEAD), BF),
             vm((HEAD, WIDTH), BF),
             vm((HEAD, HEAD), BF),
-            vm((HEAD, HEAD), BF),
+            vm((2, HEAD, HEAD), BF),
             vm((HEAD, WIDTH), BF),
             vm((ROWS, HEAD), F32),
             vm((NDEV, VX), F32),
@@ -465,7 +475,8 @@
             vm((1, WIDTH), F32),
             dma((13,)),
         ]
-        + [dma(())] * 16,
+        + [dma(()), dma((LB,))]
+        + [dma(())] * 14,
         compiler_params=pltpu.CompilerParams(collective_id=0, has_side_effects=True, vmem_limit_bytes=60 << 20),
         name="whole_step",
     )(
@@ -477,7 +488,7 @@
         out_shape=tuple(jax.ShapeDtypeStruct(shape, kind) for shape, kind in RESULTS),
         in_specs=[pl.BlockSpec(memory_space=pltpu.VMEM)] * 4,
         out_specs=(pl.BlockSpec(memory_space=pl.ANY),) * 4,
-        scratch_shapes=[dma((4,))],
+        scratch_shapes=[dma((7,))],
         name="hand_on",
     )(*[pltpu.with_memory_space_constraint(result, pltpu.VMEM) for result in results])
     return (output.reshape(LB, STEPS, WIDTH), grad_qkv, grad_out, grad_embed)

time: 39.9 us -> 39.6 us (level)
  no operation moved by 1% of the time
where the time goes in v5:
time: 39.6 us; the launch traced here: 39.5 us
  Pallas kernels  38.8 us (98%)
  between operations  0.64 us (2%)
    pallas_call x1, Pallas kernels, shards(): pl.pallas_call(kernel, out_shape=tuple((vm(shape, kind) for shape, kind i...  37.9 us
    pallas_call x1, Pallas kernels, shards(): pl.pallas_call(hand_on, out_shape=tuple((jax.ShapeDtypeStruct(shape, kind...  0.9 us

profile of v5, /device:TPU:1, one launch (start us, length us, event | category | flops | bytes accessed | tf_op | source)
XLA Modules:
  0.0 39.5 jit_solution(13630878536930520102)
XLA Ops:
  0.6 37.9 %whole_step.1 = (bf16[512,512]{1,0:T(8,128)(2,1)S(1)}, f32[16,1536]{1,0:T(8,128)S(1)}, f32[16,512]{1,0:T(8,128)S(1)}, f32[16,32]{1,0:T(8,128)S(1)}) custom-call(f32[64,4,128]{2,1,0:T(4,128)} %bitcast.10, s32[3,8]{1,0:T(4,128)} %bitcast.12, f32[3,8]{1,0:T(4,128)} %bitcast.13, s32[3,8]{1,0:T(4,128)} %bitcast.14, bf16[32,512]{1,0:T(8,128)(2,1)} %bitcast.11, ...), custom_call_target="tpu_custom_call" | custom-call | tf_op jit(solution)/shard_map/whole_step/pallas_call | solution.py:419
  38.6 0.9 %hand_on.1 = (bf16[512,512]{1,0:T(8,128)(2,1)}, f32[16,1536]{1,0:T(8,128)}, f32[16,512]{1,0:T(8,128)}, f32[16,32]{1,0:T(8,128)}) custom-call(bf16[512,512]{1,0:T(8,128)(2,1)S(1)} %get-tuple-element.12.refs_0_, f32[16,1536]{1,0:T(8,128)S(1)} %get-tuple-element.13.refs_1_, f32[16,512]{1,0:T(8,128)S(1)} %get-tuple-element.14.refs_2_, ...), custom_call_target="tpu_custom_call" | custom-call | tf_op jit(solution)/shard_map/hand_on/pallas_call | solution.py:486

commit v6 on v5

--- a/solution.py
+++ b/solution.py
@@ -23,7 +23,6 @@
 WIDTH = 512
 LOCAL_SOURCES = 4
 TERMS = 3
-VX = WIDTH + HEAD
 RESULTS = (((ROWS, WIDTH), BF), ((16, 3 * WIDTH), F32), ((16, WIDTH), F32), ((16, PATCH), F32))
 
 
@@ -65,9 +64,9 @@
     src, ids, wts, lens, we, wq, wo, forget, cot,
     stage_mix, recv_mix, glast, recv_g, row_gate, recv_r, m_local, recv_m, stage_s, stage_t, recv_s,
     rise, fade, decay, m4, mgs, mgp, u_ref, a_ref, y_ref, gcol, at, bt, ct, ctbig, gram, kk, wop, y0,
-    zall, recv_z, zrow, recv_zh, yxrow, recv_yx,
-    spare_g, spare_r, spare_m, spare_s, spare_z, spare_yx, spare_zh,
-    in_sem, mix_s, mix_r, g_s, g_r, r_s, r_r, m_s, m_r, s_s, s_r, z_s, z_r, zh_s, zh_r, yx_s, yx_r,
+    zmat, zpeer, zsum, recv_z, vxall, recv_x, zrow, recv_zh, yxrow, recv_yx,
+    spare_g, spare_r, spare_m, spare_s, spare_z, spare_x, spare_yx, spare_zh,
+    in_sem, mix_s, mix_r, g_s, g_r, r_s, r_r, m_s, m_r, s_s, s_r, zc_s, zc_r, z_s, z_r, x_s, x_r, zh_s, zh_r, yx_s, yx_r,
 ):
     ctx = lax.axis_index("ctx")
     mix = lax.axis_index("mix")
@@ -93,6 +92,10 @@
     plane_partners = [(ys[y] + xs[x] + cs[c], zs[z]) for y, x, c, z in ALL_STEPS if y == 0]
 
     place_x = lax.rem(ctx, 8)
+    all_rows = [(ys[y] * 4 + cs[c] * 16 + xs[x] * 2 + zs[z]) for y, x, c, z in ALL_STEPS]
+    own_row = ys[0] * 4 + cs[0] * 16 + xs[0] * 2 + zs[0]
+    chip_rows = [ys[y] * 2 + xs[x] * 2 + zs[z] for y, x, c, z in ALL_STEPS]
+    own_chip_row = ys[0] * 2 + xs[0] * 2 + zs[0]
     row_partners = [(xs[x] + cs[c]) for y, x, c in CTX_STEPS if y == 0]
 
     barrier = pltpu.get_barrier_semaphore()
@@ -288,6 +291,9 @@
     n = u * inv
     nb = n.astype(BF)
     dots = mm((y0[...] * u).astype(BF), ones) * (1.0 / HEAD)
+    zmat[...] = mm(nb, cot[...], TN).reshape(HEADS, 2, 16, WIDTH)
+    push(zmat.at[:, cs[1]], zpeer, zc_s, zc_r, ys[0] + xs[0] + cs[1], mix)
+
     drift = inv * (inv * dots)
     y = inv * (y0[...] - drift * ku)
     y_ref[...] = y
@@ -308,18 +314,21 @@
         kept = kept + pltpu.roll(kept, 64, 1)
         return kept + pltpu.roll(kept, 32, 1)
 
-    zall[:, :WIDTH] = mm(nb, cot[...], TN)
     v_rows = repeat(mm((n * (inv * dots)).astype(BF), nb, TN))
     x_rows = repeat(mm(m4[...], a_ref[...], TN))
-    zall[:, WIDTH:] = jnp.where(lane < 64, v_rows, x_rows)
-
-    for other, level in all_partners:
-        pltpu.make_async_remote_copy(
-            zall.at[pl.ds(other * NMIX + level, 1)], recv_z.at[pl.ds(me, 1)], z_s, z_r,
-            device_id=(other, level), device_id_type=MESH,
-        ).start()
-    spare_copy(zall.at[pl.ds(me, 1)], spare_z, z_s)
-    pltpu.make_async_copy(zall.at[pl.ds(me, 1)], recv_z.at[pl.ds(me, 1)], z_r).start()
+    vxall[...] = jnp.where(lane < 64, v_rows, x_rows)
+    pltpu.make_async_copy(zpeer, zpeer, zc_r).wait()
+    zsum[...] = (zmat[:, cs[0]] + zpeer[...]).reshape(NDEV // 2, WIDTH)
+    own_z = recv_z.at[pl.ds(own_chip_row, 1)]
+    own_x = recv_x.at[pl.ds(own_row, 1)]
+    for step, row, chip_row, partner in zip(ALL_STEPS, all_rows, chip_rows, all_partners):
+        if step[2] == 0:
+            push(zsum.at[pl.ds(chip_row, 1)], own_z, z_s, z_r, *partner)
+        push(vxall.at[pl.ds(row, 1)], own_x, x_s, x_r, *partner)
+    spare_copy(zsum.at[pl.ds(own_chip_row, 1)], spare_z, z_s)
+    spare_copy(vxall.at[pl.ds(own_row, 1)], spare_x, x_s)
+    pltpu.make_async_copy(zsum.at[pl.ds(own_chip_row, 1)], own_z, z_r).start()
+    pltpu.make_async_copy(vxall.at[pl.ds(own_row, 1)], own_x, x_r).start()
 
     out[...] = mm(nb, wop[...]).astype(BF)
 
@@ -342,31 +351,26 @@
     )
 
     pltpu.make_async_copy(recv_z, recv_z, z_r).wait()
-    row = jnp.sum(recv_z[...], axis=0, keepdims=True)
-    zrow[...] = row[:, :WIDTH]
-    mixed = row[:, WIDTH:]
-    fine = row[:, :WIDTH]
+    fine = jnp.sum(recv_z[...], axis=0, keepdims=True)
+    zrow[...] = fine
     high = fine.astype(BF)
     low = (fine - high.astype(F32)).astype(BF)
-    yv = mm(high, w_head, NT) + mm(low, w_head, NT) - mm(mixed[:, :PATCH].astype(BF), c_head)
-    xs = jnp.where(lane < 64, 0.0, mixed)
-    yxrow[:, :HEAD] = yv
-    yxrow[:, HEAD:] = xs + pltpu.roll(xs, 64, 1)
-
+    yv = mm(high, w_head, NT) + mm(low, w_head, NT)
+    pltpu.make_async_copy(recv_x, recv_x, x_r).wait()
+    mixed = jnp.sum(recv_x[...], axis=0, keepdims=True)
+    xs_sum = jnp.where(lane < 64, 0.0, mixed)
+    yxrow[:, :HEAD] = yv - mm(mixed[:, :PATCH].astype(BF), c_head)
+    yxrow[:, HEAD:] = xs_sum + pltpu.roll(xs_sum, 64, 1)
+    own_yx = recv_yx.at[pl.ds(own_row, 1)]
+    own_zh = recv_zh.at[pl.ds(lax.rem(own_row, NCTX), 1)]
     for partner in all_partners:
-        pltpu.make_async_remote_copy(
-            yxrow, recv_yx.at[pl.ds(me, 1)], yx_s, yx_r, device_id=partner, device_id_type=MESH
-        ).start()
+        push(yxrow, own_yx, yx_s, yx_r, *partner)
+    for partner in plane_partners:
+        push(zrow, own_zh, zh_s, zh_r, *partner)
     spare_copy(yxrow, spare_yx, yx_s)
-    pltpu.make_async_copy(yxrow, recv_yx.at[pl.ds(me, 1)], yx_r).start()
-    local = lax.rem(me, NCTX)
-
-    for partner in plane_partners:
-        pltpu.make_async_remote_copy(
-            zrow, recv_zh.at[pl.ds(local, 1)], zh_s, zh_r, device_id=partner, device_id_type=MESH
-        ).start()
     spare_copy(zrow, spare_zh, zh_s)
-    pltpu.make_async_copy(zrow, recv_zh.at[pl.ds(local, 1)], zh_r).start()
+    pltpu.make_async_copy(yxrow, own_yx, yx_r).start()
+    pltpu.make_async_copy(zrow, own_zh, zh_r).start()
 
     pltpu.make_async_copy(recv_zh, recv_zh, zh_r).wait()
     gout[...] = mm(c_rows, recv_zh[...].astype(BF))
@@ -392,17 +396,13 @@
     sent_mix = stage_mix.at[pl.ds(0, LB * (NMIX - 1))]
     pltpu.make_async_copy(sent_mix, sent_mix, mix_s).wait()
     for ref, sem in (
-        (recv_g, g_s), (recv_r, r_s), (recv_m, m_s), (recv_s, s_s), (recv_z, z_s), (recv_yx, yx_s), (recv_zh, zh_s)
+        (recv_g, g_s), (recv_r, r_s), (recv_m, m_s), (recv_s, s_s), (zpeer, zc_s), (recv_z, z_s), (recv_x, x_s), (recv_yx, yx_s), (recv_zh, zh_s)
     ):
         pltpu.make_async_copy(ref, ref, sem).wait()
 
 
 def hand_on(*refs):
-    moves = [(refs[i], refs[4 + i]) for i in range(1, 4)]
-    for i in range(4):
-        rows = pl.ds(i * ROWS // 4, ROWS // 4)
-        moves.append((refs[0].at[rows], refs[4].at[rows]))
-    copies = [pltpu.make_async_copy(a, b, refs[8].at[i]) for i, (a, b) in enumerate(moves)]
+    copies = [pltpu.make_async_copy(refs[i], refs[4 + i], refs[8].at[i]) for i in range(4)]
     for copy in copies:
         copy.start()
     for copy in copies:
@@ -460,8 +460,12 @@
             vm((2, HEAD, HEAD), BF),
             vm((HEAD, WIDTH), BF),
             vm((ROWS, HEAD), F32),
-            vm((NDEV, VX), F32),
-            vm((NDEV, VX), F32),
+            vm((HEADS, 2, 16, WIDTH), F32),
+            vm((HEADS, 16, WIDTH), F32),
+            vm((NDEV // 2, WIDTH), F32),
+            vm((NDEV // 2, WIDTH), F32),
+            vm((NDEV, HEAD), F32),
+            vm((NDEV, HEAD), F32),
             vm((1, WIDTH), F32),
             vm((NCTX, WIDTH), F32),
             vm((1, 2 * HEAD), F32),
@@ -470,13 +474,14 @@
             vm((LB, HEAD), F32),
             vm((8, HEAD), F32),
             vm((8, HEAD), F32),
-            vm((1, VX), F32),
+            vm((1, WIDTH), F32),
+            vm((1, HEAD), F32),
             vm((1, 2 * HEAD), F32),
             vm((1, WIDTH), F32),
             dma((13,)),
         ]
         + [dma(()), dma((LB,))]
-        + [dma(())] * 14,
+        + [dma(())] * 18,
         compiler_params=pltpu.CompilerParams(collective_id=0, has_side_effects=True, vmem_limit_bytes=60 << 20),
         name="whole_step",
     )(
@@ -488,7 +493,7 @@
         out_shape=tuple(jax.ShapeDtypeStruct(shape, kind) for shape, kind in RESULTS),
         in_specs=[pl.BlockSpec(memory_space=pltpu.VMEM)] * 4,
         out_specs=(pl.BlockSpec(memory_space=pl.ANY),) * 4,
-        scratch_shapes=[dma((7,))],
+        scratch_shapes=[dma((4,))],
         name="hand_on",
     )(*[pltpu.with_memory_space_constraint(result, pltpu.VMEM) for result in results])
     return (output.reshape(LB, STEPS, WIDTH), grad_qkv, grad_out, grad_embed)

time: 39.6 us -> 39 us (0.985)
  Pallas kernels: 38.8 us -> 38.3 us
    pallas_call x1, Pallas kernels: 37.9 us -> 37.4 us  [shards(): pl.pallas_call(kernel, out_shape=tuple((vm(shape, kind) for shape, kind i...]
where the time goes in v6:
time: 39 us; the launch traced here: 38.9 us
  Pallas kernels  38.3 us (98%)
  between operations  0.64 us (2%)
    pallas_call x1, Pallas kernels, shards(): pl.pallas_call(kernel, out_shape=tuple((vm(shape, kind) for shape, kind i...  37.4 us
    pallas_call x1, Pallas kernels, shards(): pl.pallas_call(hand_on, out_shape=tuple((jax.ShapeDtypeStruct(shape, kind...  0.86 us

profile of v6, /device:TPU:1, one launch (start us, length us, event | category | flops | bytes accessed | tf_op | source)
XLA Modules:
  0.0 38.9 jit_solution(1682056511790553039)
XLA Ops:
  0.6 37.4 %whole_step.1 = (bf16[512,512]{1,0:T(8,128)(2,1)S(1)}, f32[16,1536]{1,0:T(8,128)S(1)}, f32[16,512]{1,0:T(8,128)S(1)}, f32[16,32]{1,0:T(8,128)S(1)}) custom-call(f32[64,4,128]{2,1,0:T(4,128)} %bitcast.10, s32[3,8]{1,0:T(4,128)} %bitcast.12, f32[3,8]{1,0:T(4,128)} %bitcast.13, s32[3,8]{1,0:T(4,128)} %bitcast.14, bf16[32,512]{1,0:T(8,128)(2,1)} %bitcast.11, ...), custom_call_target="tpu_custom_call" | custom-call | tf_op jit(solution)/shard_map/whole_step/pallas_call | solution.py:419
  38.1 0.9 %hand_on.1 = (bf16[512,512]{1,0:T(8,128)(2,1)}, f32[16,1536]{1,0:T(8,128)}, f32[16,512]{1,0:T(8,128)}, f32[16,32]{1,0:T(8,128)}) custom-call(bf16[512,512]{1,0:T(8,128)(2,1)S(1)} %get-tuple-element.12.refs_0_, f32[16,1536]{1,0:T(8,128)S(1)} %get-tuple-element.13.refs_1_, f32[16,512]{1,0:T(8,128)S(1)} %get-tuple-element.14.refs_2_, ...), custom_call_target="tpu_custom_call" | custom-call | tf_op jit(solution)/shard_map/hand_on/pallas_call | solution.py:491

commit v7 on v6

--- a/solution.py
+++ b/solution.py
@@ -63,7 +63,7 @@
     out, gqkv, gout, gemb,
     src, ids, wts, lens, we, wq, wo, forget, cot,
     stage_mix, recv_mix, glast, recv_g, row_gate, recv_r, m_local, recv_m, stage_s, stage_t, recv_s,
-    rise, fade, decay, m4, mgs, mgp, u_ref, a_ref, y_ref, gcol, at, bt, ct, ctbig, gram, kk, wop, y0,
+    rise, fade, decay, m4, mgs, mgp, u_ref, mt, y_ref, gcol, at, bt, ct, ctbig, gram, kk, wop, y0,
     zmat, zpeer, zsum, recv_z, vxall, recv_x, zrow, recv_zh, yxrow, recv_yx,
     spare_g, spare_r, spare_m, spare_s, spare_z, spare_x, spare_yx, spare_zh,
     in_sem, mix_s, mix_r, g_s, g_r, r_s, r_r, m_s, m_r, s_s, s_r, zc_s, zc_r, z_s, z_r, x_s, x_r, zh_s, zh_r, yx_s, yx_r,
@@ -256,6 +256,8 @@
     inside(0, (2, 3), u_ref[pl.ds(0, STEPS)])
     scores(1)
     inside(1, range(HEADS), None)
+    for b in range(LB):
+        mt[b] = m4[pl.ds(b * STEPS, STEPS)].astype(F32).T[:PATCH].astype(BF)
     cot_load.wait()
     y0[...] = mm(cot[...], wop[...], NT)
     pltpu.make_async_copy(recv_r, recv_r, r_r).wait()
@@ -297,17 +299,23 @@
     drift = inv * (inv * dots)
     y = inv * (y0[...] - drift * ku)
     y_ref[...] = y
+    inside_x = jnp.zeros((HEAD, HEAD), F32)
+    before_x = jnp.zeros((HEAD, HEAD), F32)
     for b in range(LB):
         rows = pl.ds(b * STEPS, STEPS)
         mb = m4[rows]
         yb = y_ref[rows]
         yh = yb.astype(BF)
-        total = mm((yb * rise[b]).astype(BF), memory[b])
+        stacked = jnp.concatenate([jnp.where(heads[h], yh, jnp.zeros_like(yh)) for h in range(HEADS)], axis=0)
+        left = mm(stacked, mb, NT)
+        parts = []
         for h in range(HEADS):
-            left = mm(jnp.where(heads[h], yh, jnp.zeros_like(yh)), mb, NT)
-            left = (left * decay[b * HEADS + h]).astype(BF)
-            total = total + mm(left, jnp.where(heads[h], mb, jnp.zeros_like(mb)))
-        a_ref[rows] = total.astype(BF)
+            one = (left[h * STEPS : (h + 1) * STEPS] * decay[b * HEADS + h]).astype(BF)
+            parts.append(mm(mt[b], one).astype(BF))
+        inside_x = inside_x + mm(jnp.concatenate(parts, axis=0), mb)
+        risen = mm(mt[b], (yb * rise[b]).astype(BF))
+        risen = jnp.where(block, jnp.concatenate([risen] * HEADS, axis=0), 0.0).astype(BF)
+        before_x = before_x + mm(risen, memory[b])
 
     def repeat(square_block):
         kept = jnp.where(block, square_block, 0.0)
@@ -315,7 +323,7 @@
         return kept + pltpu.roll(kept, 32, 1)
 
     v_rows = repeat(mm((n * (inv * dots)).astype(BF), nb, TN))
-    x_rows = repeat(mm(m4[...], a_ref[...], TN))
+    x_rows = inside_x + repeat(before_x)
     vxall[...] = jnp.where(lane < 64, v_rows, x_rows)
     pltpu.make_async_copy(zpeer, zpeer, zc_r).wait()
     zsum[...] = (zmat[:, cs[0]] + zpeer[...]).reshape(NDEV // 2, WIDTH)
@@ -356,21 +364,21 @@
     high = fine.astype(BF)
     low = (fine - high.astype(F32)).astype(BF)
     yv = mm(high, w_head, NT) + mm(low, w_head, NT)
+    own_zh = recv_zh.at[pl.ds(lax.rem(own_row, NCTX), 1)]
+    for partner in plane_partners:
+        push(zrow, own_zh, zh_s, zh_r, *partner)
+    spare_copy(zrow, spare_zh, zh_s)
+    pltpu.make_async_copy(zrow, own_zh, zh_r).start()
     pltpu.make_async_copy(recv_x, recv_x, x_r).wait()
     mixed = jnp.sum(recv_x[...], axis=0, keepdims=True)
     xs_sum = jnp.where(lane < 64, 0.0, mixed)
     yxrow[:, :HEAD] = yv - mm(mixed[:, :PATCH].astype(BF), c_head)
     yxrow[:, HEAD:] = xs_sum + pltpu.roll(xs_sum, 64, 1)
     own_yx = recv_yx.at[pl.ds(own_row, 1)]
-    own_zh = recv_zh.at[pl.ds(lax.rem(own_row, NCTX), 1)]
     for partner in all_partners:
         push(yxrow, own_yx, yx_s, yx_r, *partner)
-    for partner in plane_partners:
-        push(zrow, own_zh, zh_s, zh_r, *partner)
     spare_copy(yxrow, spare_yx, yx_s)
-    spare_copy(zrow, spare_zh, zh_s)
     pltpu.make_async_copy(yxrow, own_yx, yx_r).start()
-    pltpu.make_async_copy(zrow, own_zh, zh_r).start()
 
     pltpu.make_async_copy(recv_zh, recv_zh, zh_r).wait()
     gout[...] = mm(c_rows, recv_zh[...].astype(BF))
@@ -449,7 +457,7 @@
             vm((ROWS, HEAD), BF),
             vm((ROWS, HEAD), BF),
             vm((ROWS, HEAD), F32),
-            vm((ROWS, HEAD), BF),
+            vm((LB, PATCH, STEPS), BF),
             vm((ROWS, HEAD), F32),
             vm((LB, STEPS, HEAD), F32),
             vm((HEAD, HEAD), BF),

time: 39 us -> 39.1 us (level)
  no operation moved by 1% of the time
where the time goes in v7:
time: 39.1 us; the launch traced here: 38.9 us
  Pallas kernels  38.3 us (98%)
  between operations  0.64 us (2%)
    pallas_call x1, Pallas kernels, shards(): pl.pallas_call(kernel, out_shape=tuple((vm(shape, kind) for shape, kind i...  37.4 us
    pallas_call x1, Pallas kernels, shards(): pl.pallas_call(hand_on, out_shape=tuple((jax.ShapeDtypeStruct(shape, kind...  0.86 us

profile of v7, /device:TPU:1, one launch (start us, length us, event | category | flops | bytes accessed | tf_op | source)
XLA Modules:
  0.0 38.9 jit_solution(10579668097857772836)
XLA Ops:
  0.6 37.4 %whole_step.1 = (bf16[512,512]{1,0:T(8,128)(2,1)S(1)}, f32[16,1536]{1,0:T(8,128)S(1)}, f32[16,512]{1,0:T(8,128)S(1)}, f32[16,32]{1,0:T(8,128)S(1)}) custom-call(f32[64,4,128]{2,1,0:T(4,128)} %bitcast.10, s32[3,8]{1,0:T(4,128)} %bitcast.12, f32[3,8]{1,0:T(4,128)} %bitcast.13, s32[3,8]{1,0:T(4,128)} %bitcast.14, bf16[32,512]{1,0:T(8,128)(2,1)} %bitcast.11, ...), custom_call_target="tpu_custom_call" | custom-call | tf_op jit(solution)/shard_map/whole_step/pallas_call | solution.py:427
  38.1 0.9 %hand_on.1 = (bf16[512,512]{1,0:T(8,128)(2,1)}, f32[16,1536]{1,0:T(8,128)}, f32[16,512]{1,0:T(8,128)}, f32[16,32]{1,0:T(8,128)}) custom-call(bf16[512,512]{1,0:T(8,128)(2,1)S(1)} %get-tuple-element.12.refs_0_, f32[16,1536]{1,0:T(8,128)S(1)} %get-tuple-element.13.refs_1_, f32[16,512]{1,0:T(8,128)S(1)} %get-tuple-element.14.refs_2_, ...), custom_call_target="tpu_custom_call" | custom-call | tf_op jit(solution)/shard_map/hand_on/pallas_call | solution.py:499

commit v8 on v7

--- a/solution.py
+++ b/solution.py
@@ -63,7 +63,7 @@
     out, gqkv, gout, gemb,
     src, ids, wts, lens, we, wq, wo, forget, cot,
     stage_mix, recv_mix, glast, recv_g, row_gate, recv_r, m_local, recv_m, stage_s, stage_t, recv_s,
-    rise, fade, decay, m4, mgs, mgp, u_ref, mt, y_ref, gcol, at, bt, ct, ctbig, gram, kk, wop, y0,
+    rise, fade, tall_rows, decay, m4, mgs, mgp, u_ref, mt, y_ref, gcol, at, bt, ct, ctbig, gram, kk, wop, y0,
     zmat, zpeer, zsum, recv_z, vxall, recv_x, zrow, recv_zh, yxrow, recv_yx,
     spare_g, spare_r, spare_m, spare_s, spare_z, spare_x, spare_yx, spare_zh,
     in_sem, mix_s, mix_r, g_s, g_r, r_s, r_r, m_s, m_r, s_s, s_r, zc_s, zc_r, z_s, z_r, x_s, x_r, zh_s, zh_r, yx_s, yx_r,
@@ -81,7 +81,7 @@
     moves += [(forget_hbm.at[b], forget.at[pl.ds(b * HEADS, HEADS)]) for b in range(LB)]
     copies = [pltpu.make_async_copy(a, b, in_sem.at[i]) for i, (a, b) in enumerate(moves)]
     part_loads, weight_loads, cot_load, gate_loads = copies[:7], copies[7:10], copies[10], copies[11:]
-    for copy in part_loads + gate_loads + weight_loads + [cot_load]:
+    for copy in part_loads:
         copy.start()
 
     ys = [lax.rem(ctx // 8 + d, 4) * 8 for d in range(4)]
@@ -105,6 +105,9 @@
         pl.semaphore_signal(barrier, inc=1, device_id=(ys[0] + other, mix), device_id_type=MESH)
     for base in ys[1:]:
         pl.semaphore_signal(barrier, inc=1, device_id=(base + place_x, mix), device_id_type=MESH)
+
+    for copy in gate_loads + weight_loads + [cot_load]:
+        copy.start()
 
     for load in part_loads:
         load.wait()
@@ -203,12 +206,13 @@
     spare_copy(row_gate, spare_r, r_s)
 
     spread = (lax.rem(iota((HEAD, HEAD), 0), PATCH) == lax.rem(iota((HEAD, HEAD), 1), PATCH)).astype(BF)
-    pick = (iota((STEPS, 64), 0) // 4 == iota((STEPS, 64), 1)).astype(BF)
     mine = lax.rem(iota((STEPS, HEAD), 0), 4) == iota((STEPS, HEAD), 1) // PATCH
     for b in range(LB):
         pltpu.make_async_copy(recv_mix.at[b], recv_mix.at[b], mix_r.at[b]).wait()
-        packed = ((recv_mix[b, 0] + recv_mix[b, 1]) + (recv_mix[b, 2] + recv_mix[b, 3])).astype(BF)
-        lone = jnp.where(mine, mm(pick, packed), 0.0).astype(BF)
+        packed = ((recv_mix[b, 0] + recv_mix[b, 1]) + (recv_mix[b, 2] + recv_mix[b, 3]))
+        for k in range(4):
+            tall_rows[b, pl.ds(k, 64, stride=4)] = packed
+        lone = jnp.where(mine, tall_rows[b], 0.0).astype(BF)
         rows = mm(lone, spread)
         m4[pl.ds(b * STEPS, STEPS)] = rows.astype(BF)
         faded = (rows * fade[b]).astype(BF)
@@ -325,14 +329,17 @@
     v_rows = repeat(mm((n * (inv * dots)).astype(BF), nb, TN))
     x_rows = inside_x + repeat(before_x)
     vxall[...] = jnp.where(lane < 64, v_rows, x_rows)
+    own_z = recv_z.at[pl.ds(own_chip_row, 1)]
+    own_x = recv_x.at[pl.ds(own_row, 1)]
+    for row, partner in zip(all_rows[:40], all_partners):
+        push(vxall.at[pl.ds(row, 1)], own_x, x_s, x_r, *partner)
     pltpu.make_async_copy(zpeer, zpeer, zc_r).wait()
     zsum[...] = (zmat[:, cs[0]] + zpeer[...]).reshape(NDEV // 2, WIDTH)
-    own_z = recv_z.at[pl.ds(own_chip_row, 1)]
-    own_x = recv_x.at[pl.ds(own_row, 1)]
-    for step, row, chip_row, partner in zip(ALL_STEPS, all_rows, chip_rows, all_partners):
+    for n, (step, row, chip_row, partner) in enumerate(zip(ALL_STEPS, all_rows, chip_rows, all_partners)):
         if step[2] == 0:
             push(zsum.at[pl.ds(chip_row, 1)], own_z, z_s, z_r, *partner)
-        push(vxall.at[pl.ds(row, 1)], own_x, x_s, x_r, *partner)
+        if n >= 40:
+            push(vxall.at[pl.ds(row, 1)], own_x, x_s, x_r, *partner)
     spare_copy(zsum.at[pl.ds(own_chip_row, 1)], spare_z, z_s)
     spare_copy(vxall.at[pl.ds(own_row, 1)], spare_x, x_s)
     pltpu.make_async_copy(zsum.at[pl.ds(own_chip_row, 1)], own_z, z_r).start()
@@ -450,6 +457,7 @@
             vm((ROW, 8, HEAD), F32),
             vm((8, HEAD), F32),
             vm((PLANES, ROW, 8, HEAD), F32),
+            vm((LB, STEPS, HEAD), F32),
             vm((LB, STEPS, HEAD), F32),
             vm((LB, STEPS, HEAD), F32),
             vm((LB * HEADS, STEPS, STEPS), F32),

time: 39.1 us -> 38.9 us (level)
  no operation moved by 1% of the time
where the time goes in v8:
time: 38.9 us; the launch traced here: 38.8 us
  Pallas kernels  38.1 us (98%)
  between operations  0.64 us (2%)
    pallas_call x1, Pallas kernels, shards(): pl.pallas_call(kernel, out_shape=tuple((vm(shape, kind) for shape, kind i...  37.3 us
    pallas_call x1, Pallas kernels, shards(): pl.pallas_call(hand_on, out_shape=tuple((jax.ShapeDtypeStruct(shape, kind...  0.86 us

profile of v8, /device:TPU:1, one launch (start us, length us, event | category | flops | bytes accessed | tf_op | source)
XLA Modules:
  0.0 38.8 jit_solution(9115795585796622876)
XLA Ops:
  0.6 37.3 %whole_step.1 = (bf16[512,512]{1,0:T(8,128)(2,1)S(1)}, f32[16,1536]{1,0:T(8,128)S(1)}, f32[16,512]{1,0:T(8,128)S(1)}, f32[16,32]{1,0:T(8,128)S(1)}) custom-call(f32[64,4,128]{2,1,0:T(4,128)} %bitcast.10, s32[3,8]{1,0:T(4,128)} %bitcast.12, f32[3,8]{1,0:T(4,128)} %bitcast.13, s32[3,8]{1,0:T(4,128)} %bitcast.14, bf16[32,512]{1,0:T(8,128)(2,1)} %bitcast.11, ...), custom_call_target="tpu_custom_call" | custom-call | tf_op jit(solution)/shard_map/whole_step/pallas_call | solution.py:434
  37.9 0.9 %hand_on.1 = (bf16[512,512]{1,0:T(8,128)(2,1)}, f32[16,1536]{1,0:T(8,128)}, f32[16,512]{1,0:T(8,128)}, f32[16,32]{1,0:T(8,128)}) custom-call(bf16[512,512]{1,0:T(8,128)(2,1)S(1)} %get-tuple-element.12.refs_0_, f32[16,1536]{1,0:T(8,128)S(1)} %get-tuple-element.13.refs_1_, f32[16,512]{1,0:T(8,128)S(1)} %get-tuple-element.14.refs_2_, ...), custom_call_target="tpu_custom_call" | custom-call | tf_op jit(solution)/shard_map/hand_on/pallas_call | solution.py:507
